TPU v7x, 256 devices: a whole 4x4x8 slice. The times are simulated.
256 devices in a mesh: leaf: 4 (over y), frow: 16 (over z, x_lo), fcol: 4 (over x_hi, core).
Axes of the slice: x: 4 (x_hi: 2, x_lo: 2; x = x_hi * 2 + x_lo), y: 4, z: 8, core: 2. Of those that a mesh axis runs over, the one named last changes fastest.
Arguments:
- child_fronts: float32 [4, 4096, 4096], P('leaf', 'frow', 'fcol'), may hold values from -20 to 120, as said below
- parent_front: float32 [4096, 4096], P('frow', 'fcol'), may hold values from -20 to 120, as said below
- block_maps: int32 [4, 32], P('leaf'), may hold values from 0 to 31, as said below
Outputs:
- child_factors: float32 [4, 4096, 4096], P('leaf', 'frow', 'fcol')
- parent_factor: float32 [4096, 4096], P('frow', 'fcol')
Inputs may be any that keep to these rules, and one draw needn't show every extreme that they name: Each row block_maps[l] is a permutation of the block numbers that keeps every block inside its group of 2 consecutive blocks: block_maps[l, i] // 2 == i // 2. `child_fronts`: every child front is symmetric positive definite. `parent_front`: the parent front is symmetric positive definite.
All inputs are finite; a program needn't handle non-finite values.
Results may differ from a plain program's by a relative error of at most 0.0001.
Values sent between devices are 32-bit elements; how exact they have to be, the bound alone decides.
No kernel may reach another device: no remote copies, remote signals or barrier semaphores. Data moves between devices by JAX's collectives and lax.ppermute only.
A program may use at most 64 MiB of HBM per device.

v0:
```python
import jax
import jax.numpy as jnp
from jax import lax
from jax.experimental import pallas as pl
from jax.experimental.pallas import tpu as pltpu
from jax.sharding import PartitionSpec as P


BLOCK = 128
PIVOTS = 256
PLANE = ("frow", "fcol")
ROWS = 16
COLS = 4
HIGHEST = lax.Precision.HIGHEST
VMEM = pl.BlockSpec(memory_space=pltpu.VMEM)
SMEM = pl.BlockSpec(memory_space=pltpu.SMEM)


def mm(a, b):
    return lax.dot_general(
        a, b, (((1,), (0,)), ((), ())), precision=HIGHEST, preferred_element_type=jnp.float32
    )


def mm_t(a, b):
    return lax.dot_general(
        a, b, (((1,), (1,)), ((), ())), precision=HIGHEST, preferred_element_type=jnp.float32
    )


def halves(x):
    high = x.astype(jnp.bfloat16)
    return high, (x - high.astype(jnp.float32)).astype(jnp.bfloat16)


def product_t(a, b):
    dot = lambda x, y: lax.dot_general(
        x, y, (((1,), (1,)), ((), ())), preferred_element_type=jnp.float32
    )
    (ah, al), (bh, bl) = a, b
    return dot(ah, bh) + (dot(ah, bl) + dot(al, bh))


def f32(*shape):
    return jax.ShapeDtypeStruct(shape, jnp.float32)


def eight_columns(groups, start):
    lane = lax.broadcasted_iota(jnp.int32, (8, BLOCK), 1)
    sub = lax.broadcasted_iota(jnp.int32, (8, BLOCK), 0)
    spread = lambda v: jnp.broadcast_to(v, (8, BLOCK))
    here = start // 8
    inside = (lane >= start) & (lane < start + 8)
    x = groups[here]
    column = [spread(x[:, start + k : start + k + 1]) for k in range(8)]
    s = [[spread(column[k][i : i + 1]) if k <= i else None for k in range(8)] for i in range(8)]
    unit = jnp.where(inside, jnp.where(lane - start == sub, 1.0, 0.0), x)
    line = [spread(unit[k : k + 1]) for k in range(8)]
    inv = [None] * 8
    low = [[None] * 8 for _ in range(8)]
    forward = [None] * 8
    for k in range(8):
        inv[k] = 1.0 / s[k][k]
        for i in range(k + 1, 8):
            low[i][k] = s[i][k] * inv[k]
        for i in range(k + 1, 8):
            for q in range(k + 1, i + 1):
                s[i][q] = s[i][q] - low[i][k] * s[q][k]
        t = line[k]
        for q in range(k):
            t = t - low[k][q] * forward[q]
        forward[k] = t
    back = [None] * 8
    for k in reversed(range(8)):
        t = inv[k] * forward[k]
        for i in range(k + 1, 8):
            t = t - low[i][k] * back[i]
        back[k] = t
    for g in range(here + 1, BLOCK // 8):
        rows = groups[g]
        parts = [spread(rows[:, start + k : start + k + 1]) * back[k] for k in range(8)]
        while len(parts) > 1:
            parts = [parts[i] + parts[i + 1] for i in range(0, len(parts), 2)]
        groups[g] = jnp.where(inside, 0.0, rows) - parts[0]
    own = forward[0] * jnp.sqrt(inv[0])
    for k in range(1, 8):
        own = jnp.where(sub == k, forward[k] * jnp.sqrt(inv[k]), own)
    groups[here] = own


def inverse_factors(blocks):
    split = [[b[8 * g : 8 * g + 8] for g in range(BLOCK // 8)] for b in blocks]
    for start in range(0, BLOCK, 8):
        for groups in split:
            eight_columns(groups, start)
    row, col = square()
    return [jnp.where(col <= row, jnp.concatenate(groups, axis=0), 0.0) for groups in split]


def square():
    shape = (BLOCK, BLOCK)
    return lax.broadcasted_iota(jnp.int32, shape, 0), lax.broadcasted_iota(jnp.int32, shape, 1)


def pack_body(front, parent, pivots, rows, *scattered):
    leaf = lax.axis_index("leaf")
    row, col = square()
    a11 = front[0, :BLOCK, :BLOCK]
    a22 = front[0, BLOCK:, BLOCK:]
    pivots[:BLOCK] = jnp.where(col <= row, a11, a22)
    pivots[BLOCK:PIVOTS] = front[0, BLOCK:, :BLOCK]
    pivots[PIVOTS : PIVOTS + BLOCK] = parent[:BLOCK]
    diag = jnp.sum(jnp.where(row == col, a22, 0.0), axis=0, keepdims=True)
    pivots[PIVOTS + BLOCK :] = jnp.broadcast_to(diag, (8, BLOCK))
    rows[:, :PIVOTS] = front[0]
    rows[:, PIVOTS:] = parent[...]
    for j, out in enumerate(scattered):
        out[:64] = front[0, 64 * j : 64 * j + 64]
        at_row = pl.multiple_of(64 * leaf + 16 * j, 8)
        out[64:, :BLOCK] = parent[pl.ds(at_row, 8)]
        out[64:, BLOCK:] = parent[pl.ds(at_row + 8, 8)]


def pack(front, parent):
    return pl.pallas_call(
        pack_body,
        grid=(1,),
        in_specs=[
            pl.BlockSpec((1, PIVOTS, PIVOTS), lambda i: (0, 0, 0)),
            pl.BlockSpec((PIVOTS, BLOCK), lambda i: (0, 0)),
        ],
        out_specs=[VMEM] * 6,
        out_shape=[f32(392, BLOCK), f32(256, 384)] + [f32(72, PIVOTS)] * 4,
        name="pack",
    )(front, parent)


def factor_body(pivots, k, k_inv, kp, kp_inv):
    row, col = square()
    both = pivots[:BLOCK]
    low = jnp.where(col <= row, both, 0.0)
    a11 = low + jnp.where(col < row, low, 0.0).T
    high = jnp.where(col > row, both, 0.0)
    diag = jnp.broadcast_to(pivots[PIVOTS + BLOCK : PIVOTS + BLOCK + 1], (BLOCK, BLOCK))
    a22 = high + high.T + jnp.where(row == col, diag, 0.0)
    a21 = pivots[BLOCK:PIVOTS]
    ap = pivots[PIVOTS : PIVOTS + BLOCK]
    (k1_inv,) = inverse_factors([a11])
    k21 = mm_t(a21, k1_inv)
    s22 = a22 - mm_t(k21, k21)
    k2_inv, parent_inv = inverse_factors([s22, ap])
    zero = jnp.zeros((BLOCK, BLOCK), jnp.float32)
    k_inv[:BLOCK, :BLOCK] = k1_inv
    k_inv[:BLOCK, BLOCK:] = zero
    k_inv[BLOCK:, :BLOCK] = -mm(k2_inv, mm(k21, k1_inv))
    k_inv[BLOCK:, BLOCK:] = k2_inv
    k[:BLOCK, :BLOCK] = jnp.where(col <= row, mm_t(a11, k1_inv), 0.0)
    k[:BLOCK, BLOCK:] = zero
    k[BLOCK:, :BLOCK] = k21
    k[BLOCK:, BLOCK:] = jnp.where(col <= row, mm_t(s22, k2_inv), 0.0)
    kp_inv[...] = parent_inv
    kp[...] = jnp.where(col <= row, mm_t(ap, parent_inv), 0.0)


def factor(pivots):
    return pl.pallas_call(
        factor_body,
        in_specs=[VMEM],
        out_specs=[VMEM] * 4,
        out_shape=[f32(PIVOTS, PIVOTS)] * 2 + [f32(BLOCK, BLOCK)] * 2,
        name="factor",
    )(pivots)


def raw_columns(gathered):
    return jnp.concatenate([gathered[j, :64] for j in range(4)], axis=0)


def contribute_body(
    maps, rows, gathered, k_inv, kp, kp_inv, front, parent, *rest
):
    outs, (lines_high, lines_low, columns, value) = rest[:4], rest[4:]
    leaf, r, c = lax.axis_index("leaf"), lax.axis_index("frow"), lax.axis_index("fcol")
    i = pl.program_id(0)
    kept_rows = jnp.where(r > 0, 1.0, 0.0)
    turn = maps[0, 2 * r] % 2

    @pl.when(i == 0)
    def _():
        b = mm_t(rows[:, :PIVOTS], k_inv[...]) * kept_rows
        bp = mm_t(rows[:, PIVOTS:], kp_inv[...])
        for h in range(2):
            block = slice(h * BLOCK, (h + 1) * BLOCK)
            to = pl.multiple_of((h + turn) % 2 * BLOCK, BLOCK)
            lines_high[pl.ds(to, BLOCK), :PIVOTS], lines_low[pl.ds(to, BLOCK), :PIVOTS] = halves(b[block])
            mine = bp[block] * kept_rows if h == 0 else bp[block]
            lines_high[block, PIVOTS:], lines_low[block, PIVOTS:] = halves(mine)
        columns[:, PIVOTS:] = jnp.zeros((256, BLOCK), jnp.float32)

    pair = lax.broadcasted_iota(jnp.int32, (1, BLOCK), 1)
    kept = jnp.where((c > 0) | (i > 0), 1.0, 0.0)
    swap = maps[0, 2 * (4 * c + i)] % 2
    own = mm_t(raw_columns(gathered), k_inv[...])
    for h in range(2):
        to = pl.multiple_of((h + swap) % 2 * BLOCK, BLOCK)
        columns[pl.ds(to, BLOCK), :PIVOTS] = own[h * BLOCK : (h + 1) * BLOCK] * kept
    strip = jnp.concatenate(
        [gathered[j, 64:, half : half + BLOCK] for j in range(4) for half in (0, BLOCK)], axis=0
    )
    pivot_strip = (c == 0) & (i == 0) & (leaf < 2)
    to = pl.multiple_of(64 * leaf, 64)
    columns[pl.ds(to, 64), PIVOTS:] = mm_t(strip, kp_inv[...]) * jnp.where(pivot_strip, 0.0, 1.0)
    update = product_t((lines_high[...], lines_low[...]), halves(columns[...]))
    for h in range(2):
        from_row = pl.multiple_of((h + turn) % 2 * BLOCK, BLOCK)
        block = slice(h * BLOCK, (h + 1) * BLOCK)
        for g in range(2):
            from_col = pl.multiple_of((g + swap) % 2 * BLOCK, BLOCK)
            strips = slice(g * BLOCK, (g + 1) * BLOCK)
            mine = (2 * g + pair // 64) == leaf
            child = front[0, pl.ds(from_row, BLOCK), pl.ds(from_col, BLOCK)] * (kept_rows * kept)
            theirs = parent[block, strips]
            if h == 0:
                theirs = theirs * kept_rows
            value[block, strips] = child + jnp.where(mine, theirs, 0.0) - update[block, strips]

    @pl.when((c == 0) & (i == 0))
    def _():
        mine = pair // 64 == leaf
        bp = mm_t(rows[:, PIVOTS:], kp_inv[...])
        top = jnp.where(r == 0, kp[...], bp[:BLOCK])
        value[:BLOCK, :BLOCK] = jnp.where(mine, top, 0.0)
        value[BLOCK:, :BLOCK] = jnp.where(mine, bp[BLOCK:], 0.0)

    for half, bit in enumerate(first_bits(leaf)):
        for out, at_row in ((outs[2 * half], 1 - bit), (outs[2 * half + 1], bit)):
            out[...] = value[pl.ds(pl.multiple_of(BLOCK * half + 64 * at_row, 64), 64)]


def first_bits(leaf):
    return jnp.where((leaf == 1) | (leaf == 2), 1, 0), leaf // 2


def whole(*shape):
    return pl.BlockSpec(shape, lambda i: (0,) * len(shape))


GATHERED = pl.BlockSpec((4, 72, PIVOTS), lambda i: (i, 0, 0))
FRONT = pl.BlockSpec((1, 256, 256), lambda i: (0, 0, i))
PARENT = pl.BlockSpec((256, 256), lambda i: (0, i))


def contribute(maps, rows, gathered, k_inv, kp, kp_inv, front, parent):
    return pl.pallas_call(
        contribute_body,
        grid=(4,),
        in_specs=[
            SMEM,
            whole(256, 384),
            GATHERED,
            whole(PIVOTS, PIVOTS),
            whole(BLOCK, BLOCK),
            whole(BLOCK, BLOCK),
            FRONT,
            PARENT,
        ],
        out_specs=[pl.BlockSpec((64, 256), lambda i: (0, i))] * 4,
        out_shape=[f32(64, 1024)] * 4,
        scratch_shapes=[
            pltpu.VMEM((256, 384), jnp.bfloat16),
            pltpu.VMEM((256, 384), jnp.bfloat16),
            pltpu.VMEM((256, 384), jnp.float32),
            pltpu.VMEM((256, 256), jnp.float32),
        ],
        name="contribute",
    )(maps, rows, gathered, k_inv, kp, kp_inv, front, parent)


def finish_body(rows, gathered, k, k_inv, front, out, b_rows, high, low):
    r, c = lax.axis_index("frow"), lax.axis_index("fcol")
    i = pl.program_id(0)

    @pl.when(i == 0)
    def _():
        b = mm_t(rows[:, :PIVOTS], k_inv[...])
        b_rows[...] = b
        high[...], low[...] = halves(b)

    @pl.when(r == 0)
    def _():
        out[...] = jnp.zeros_like(out)

    @pl.when(r > 0)
    def _():
        own = mm_t(raw_columns(gathered), k_inv[...])
        out[0] = front[0] - product_t((high[...], low[...]), halves(own))

    @pl.when((c == 0) & (i == 0))
    def _():
        out[0] = jnp.where(r == 0, k[...], b_rows[...])


def finish(rows, gathered, k, k_inv, front):
    return pl.pallas_call(
        finish_body,
        grid=(4,),
        in_specs=[
            whole(256, 384),
            GATHERED,
            whole(PIVOTS, PIVOTS),
            whole(PIVOTS, PIVOTS),
            FRONT,
        ],
        out_specs=FRONT,
        out_shape=f32(1, 256, 1024),
        scratch_shapes=[
            pltpu.VMEM((256, 256), jnp.float32),
            pltpu.VMEM((256, 256), jnp.bfloat16),
            pltpu.VMEM((256, 256), jnp.bfloat16),
        ],
        cost_estimate=pl.CostEstimate(flops=1 << 31, bytes_accessed=4 << 20, transcendentals=0),
        name="finish",
    )(rows, gathered, k, k_inv, front)


def at(r, c):
    return r * COLS + c


def spread_rows(x, r, steps):
    for step in steps:
        pairs = [(at(q, 0), at(q + step, 0)) for q in range(0, ROWS, 2 * step)]
        got = lax.ppermute(x, PLANE, pairs)
        x = jnp.where(r % (2 * step) == step, got, x)
    return x


def spread_far(x, c):
    got = lax.ppermute(x, PLANE, [(at(q, 0), at(q, 2)) for q in range(ROWS)])
    return jnp.where(c == 2, got, x)


def spread_core(x, c):
    got = lax.ppermute(x, PLANE, [(at(q, k), at(q, k + 1)) for q in range(ROWS) for k in (0, 2)])
    return jnp.where(c % 2 == 1, got, x)


def scatter_columns(scattered):
    piece = None
    for j, sent in enumerate(scattered):
        pairs = [(at(4 * k + i, 0), at(4 * i + j, k)) for k in range(COLS) for i in range(4)]
        got = lax.ppermute(sent, PLANE, pairs)
        piece = got if piece is None else piece + got
    return piece


def gather_columns(piece):
    copies = jnp.broadcast_to(piece[None], (ROWS, 72, PIVOTS))
    return lax.all_to_all(copies, "frow", 0, 0, tiled=True)


def sum_over_leaf(parts, leaf):
    near = [(0, 1), (1, 0), (2, 3), (3, 2)]
    far = [(0, 3), (3, 0), (1, 2), (2, 1)]
    upper, lower = first_bits(leaf)
    sends, keeps = parts[0::2], parts[1::2]
    pairs = ((near, far), (far, near))
    first = (upper, lower)
    second = (leaf // 2, leaf % 2)

    def exchange(xs, turn):
        return [lax.ppermute(x, "leaf", p[turn]) for x, p in zip(xs, pairs)]

    def ordered(bit, mine, got):
        return jnp.where(bit == 0, jnp.concatenate([mine, got]), jnp.concatenate([got, mine]))

    got = exchange(sends, 0)
    sums = [x + y for x, y in zip(keeps, got)]
    small = 32
    cut = lambda x, i: lax.dynamic_slice_in_dim(x, i * small, small)
    got = exchange([cut(x, 1 - b) for x, b in zip(sums, second)], 1)
    done = [cut(x, b) + y for x, b, y in zip(sums, second, got)]
    got = exchange(done, 1)
    halved = [ordered(b, x, y) for b, x, y in zip(second, done, got)]
    got = exchange(halved, 0)
    return jnp.concatenate([ordered(b, x, y) for b, x, y in zip(first, halved, got)])


def per_device(child_fronts, parent_front, block_maps):
    leaf = lax.axis_index("leaf")
    r = lax.axis_index("frow")
    c = lax.axis_index("fcol")
    pivots, rows, *scattered = pack(child_fronts, parent_front)
    pivots = spread_rows(pivots, r, (8, 4, 2))
    rows = spread_far(rows, c)
    piece = scatter_columns(scattered)
    gathered = gather_columns(piece)
    pivots = spread_rows(pivots, r, (1,))
    pivots = spread_far(pivots, c)
    pivots = spread_core(pivots, c)
    rows = spread_core(rows, c)
    k, k_inv, kp, kp_inv = factor(pivots)
    parts = contribute(
        block_maps, rows, gathered, k_inv, kp, kp_inv, child_fronts, parent_front
    )
    parent_done = sum_over_leaf(parts, leaf)
    return finish(rows, gathered, k, k_inv, child_fronts), parent_done


def solution(mesh):
    return jax.shard_map(
        per_device,
        mesh=mesh,
        in_specs=(P("leaf", "frow", "fcol"), P("frow", "fcol"), P("leaf", None)),
        out_specs=(P("leaf", "frow", "fcol"), P("frow", "fcol")),
        check_vma=False,
    )
```

profile of v0, /device:TPU:54, one launch (start us, length us, event | category | flops | bytes accessed | tf_op | source)
XLA Modules:
  0.0 126.6 jit_solution(1397359873365312513)
XLA Ops:
  0.6 2.0 %pack.1 = (f32[392,128]{1,0:T(8,128)}, f32[256,384]{1,0:T(8,128)}, f32[72,256]{1,0:T(8,128)}, f32[72,256]{1,0:T(8,128)}, f32[72,256]{1,0:T(8,128)}, /*index=5*/f32[72,256]{1,0:T(8,128)}) custom-call(f32[1,256,1024]{2,1,0:T(8,128)} %front.5, f32[256,1024]{1,0:T(8,128)} %parent.3), custom_call_target="tpu_custom_call" | custom-call | tf_op jit(solution)/shard_map/pack/pallas_call | solution.py:125
  3.3 1.3 %collective-permute-start.5 = (f32[72,256]{1,0:T(8,128)}, f32[72,256]{1,0:T(8,128)S(1)}, u32[]{:S(2)}, u32[]{:S(2)}) collective-permute-start(f32[72,256]{1,0:T(8,128)} %get-tuple-element.20), channel_id=1, source_target_pairs={{0,12},{4,28},{8,44},{12,60},{16,13},{20,29},{24,45},{28,61},{32,1... | collective-permute-start | bytes 221192 | tf_op jit(solution)/shard_map/ppermute | solution.py:352
  8.3 6.9 %collective-permute-done.5 = f32[72,256]{1,0:T(8,128)S(1)} collective-permute-done((f32[72,256]{1,0:T(8,128)}, f32[72,256]{1,0:T(8,128)S(1)}, u32[]{:S(2)}, u32[]{:S(2)}) %collective-permute-start.5) | collective-permute-done | bytes 73760 | tf_op jit(solution)/shard_map/ppermute | solution.py:352
  15.2 1.1 broadcast_in_dim.2
  16.3 11.8 %all-to-all-start = ((f32[16,72,256]{2,1,0:T(8,128)}), f32[16,72,256]{2,1,0:T(8,128)S(1)}, u32[]{:S(2)}, u32[]{:S(2)}) async-start(f32[16,72,256]{2,1,0:T(8,128)} %broadcast_in_dim.2), calls=%async_computation | async-start | bytes 2359296 | tf_op jit(solution)/shard_map/all_to_all | solution.py:359
  29.7 1.3 %collective-permute-start = (f32[256,384]{1,0:T(8,128)S(1)}, f32[256,384]{1,0:T(8,128)S(1)}, u32[]{:S(2)}, u32[]{:S(2)}) collective-permute-start(f32[256,384]{1,0:T(8,128)S(1)} %copy-done.1), channel_id=1, source_target_pairs={{0,2},{4,6},{8,10},{12,14},{16,18},{20,22},{24,26},{28,30},{32,34}... | collective-permute-start | bytes 1179656 | tf_op jit(solution)/shard_map/ppermute | solution.py:339
  31.1 1.3 %collective-permute-start.10 = (f32[392,128]{1,0:T(8,128)S(1)}, f32[392,128]{1,0:T(8,128)S(1)}, u32[]{:S(2)}, u32[]{:S(2)}) collective-permute-start(f32[392,128]{1,0:T(8,128)S(1)} %broadcast_select_fusion.5), channel_id=1, source_target_pairs={{0,2},{4,6},{8,10},{12,14},{16,18},{20,22},{24,26},{28,30},{32,34}... | collective-permute-start | bytes 602120 | tf_op jit(solution)/shard_map/ppermute | solution.py:339
  32.4 10.1 %collective-permute-done = f32[256,384]{1,0:T(8,128)S(1)} collective-permute-done((f32[256,384]{1,0:T(8,128)S(1)}, f32[256,384]{1,0:T(8,128)S(1)}, u32[]{:S(2)}, u32[]{:S(2)}) %collective-permute-start) | collective-permute-done | bytes 393248 | tf_op jit(solution)/shard_map/ppermute | solution.py:339
  42.6 1.3 %collective-permute-start.1 = (f32[256,384]{1,0:T(8,128)S(1)}, f32[256,384]{1,0:T(8,128)S(1)}, u32[]{:S(2)}, u32[]{:S(2)}) collective-permute-start(f32[256,384]{1,0:T(8,128)S(1)} %broadcast_select_fusion), channel_id=1, source_target_pairs={{0,1},{2,3},{4,5},{6,7},{8,9},{10,11},{12,13},{14,15},{16,17},{18,... | collective-permute-start | bytes 1179656 | tf_op jit(solution)/shard_map/ppermute | solution.py:344
  43.9 24.1 %collective-permute-done.10 = f32[392,128]{1,0:T(8,128)S(1)} collective-permute-done((f32[392,128]{1,0:T(8,128)S(1)}, f32[392,128]{1,0:T(8,128)S(1)}, u32[]{:S(2)}, u32[]{:S(2)}) %collective-permute-start.10) | collective-permute-done | bytes 200736 | tf_op jit(solution)/shard_map/ppermute | solution.py:339
  68.0 1.3 %collective-permute-start.11 = (f32[392,128]{1,0:T(8,128)S(1)}, f32[392,128]{1,0:T(8,128)S(1)}, u32[]{:S(2)}, u32[]{:S(2)}) collective-permute-start(f32[392,128]{1,0:T(8,128)S(1)} %broadcast_select_fusion.6), channel_id=1, source_target_pairs={{0,1},{2,3},{4,5},{6,7},{8,9},{10,11},{12,13},{14,15},{16,17},{18,... | collective-permute-start | bytes 602120 | tf_op jit(solution)/shard_map/ppermute | solution.py:344
  71.1 12.9 %factor.1 = (f32[256,256]{1,0:T(8,128)}, f32[256,256]{1,0:T(8,128)}, f32[128,128]{1,0:T(8,128)}, f32[128,128]{1,0:T(8,128)}) custom-call(f32[392,128]{1,0:T(8,128)} %broadcast_select_fusion.7.pivots), custom_call_target="tpu_custom_call" | custom-call | tf_op jit(solution)/shard_map/factor/pallas_call | solution.py:166
  84.0 1.0 copy-done
  85.0 7.4 %contribute.1 = (f32[64,1024]{1,0:T(8,128)}, f32[64,1024]{1,0:T(8,128)}, f32[64,1024]{1,0:T(8,128)}, f32[64,1024]{1,0:T(8,128)}) custom-call(s32[1,32]{1,0:T(1,128)} %maps.1, f32[256,384]{1,0:T(8,128)} %broadcast_select_fusion.1.rows, f32[16,72,256]{2,1,0:T(8,128)} %copy-done, f32[256,256]{1,0:T(8,128)} %get-tuple-element.23.k_inv, ...), custom_call_target="tpu_custom_call" | custom-call | tf_op jit(solution)/shard_map/contribute/pallas_call | solution.py:254
  92.9 1.1 collective-permute-start.12
  94.0 7.3 %collective-permute-done.16 = f32[64,1024]{1,0:T(8,128)S(1)} collective-permute-done((f32[64,1024]{1,0:T(8,128)}, f32[64,1024]{1,0:T(8,128)S(1)}, u32[]{:S(2)}, u32[]{:S(2)}) %collective-permute-start.16) | collective-permute-done | bytes 262176 | tf_op jit(solution)/shard_map/ppermute | solution.py:372
  102.3 2.8 %collective-permute-start.17 = (f32[32,1024]{1,0:T(8,128)S(1)}, f32[32,1024]{1,0:T(8,128)S(1)}, u32[]{:S(2)}, u32[]{:S(2)}) collective-permute-start(f32[32,1024]{1,0:T(8,128)S(1)} %constant_dynamic-slice_fusion), channel_id=1, source_target_pairs={{0,64},{64,0},{128,192},{192,128},{1,65},{65,1},{129,193},{193,129... | collective-permute-start | bytes 393224 | tf_op jit(solution)/shard_map/ppermute | solution.py:372
  105.2 3.0 %collective-permute-done.17 = f32[32,1024]{1,0:T(8,128)S(1)} collective-permute-done((f32[32,1024]{1,0:T(8,128)S(1)}, f32[32,1024]{1,0:T(8,128)S(1)}, u32[]{:S(2)}, u32[]{:S(2)}) %collective-permute-start.17) | collective-permute-done | bytes 131104 | tf_op jit(solution)/shard_map/ppermute | solution.py:372
  108.2 1.9 %collective-permute-start.18 = (f32[32,1024]{1,0:T(8,128)S(1)}, f32[32,1024]{1,0:T(8,128)S(1)}, u32[]{:S(2)}, u32[]{:S(2)}) collective-permute-start(f32[32,1024]{1,0:T(8,128)S(1)} %dynamic-slice_add_fusion), channel_id=1, source_target_pairs={{0,64},{64,0},{128,192},{192,128},{1,65},{65,1},{129,193},{193,129... | collective-permute-start | bytes 393224 | tf_op jit(solution)/shard_map/ppermute | solution.py:372
  110.3 3.0 %collective-permute-done.18 = f32[32,1024]{1,0:T(8,128)S(1)} collective-permute-done((f32[32,1024]{1,0:T(8,128)S(1)}, f32[32,1024]{1,0:T(8,128)S(1)}, u32[]{:S(2)}, u32[]{:S(2)}) %collective-permute-start.18) | collective-permute-done | bytes 131104 | tf_op jit(solution)/shard_map/ppermute | solution.py:372
  113.4 3.2 %collective-permute-done.14 = f32[32,1024]{1,0:T(8,128)S(1)} collective-permute-done((f32[32,1024]{1,0:T(8,128)S(1)}, f32[32,1024]{1,0:T(8,128)S(1)}, u32[]{:S(2)}, u32[]{:S(2)}) %collective-permute-start.14) | collective-permute-done | bytes 131104 | tf_op jit(solution)/shard_map/ppermute | solution.py:372
  116.7 2.6 %collective-permute-start.15 = (f32[64,1024]{1,0:T(8,128)S(1)}, f32[64,1024]{1,0:T(8,128)S(1)}, u32[]{:S(2)}, u32[]{:S(2)}) collective-permute-start(f32[64,1024]{1,0:T(8,128)S(1)} %maximum_select_fusion.2), channel_id=1, source_target_pairs={{0,64},{64,0},{128,192},{192,128},{1,65},{65,1},{129,193},{193,129... | collective-permute-start | bytes 786440 | tf_op jit(solution)/shard_map/ppermute | solution.py:372
  119.2 6.2 %finish.1 = f32[1,256,1024]{2,1,0:T(8,128)} custom-call(f32[256,384]{1,0:T(8,128)} %broadcast_select_fusion.1.rows, f32[16,72,256]{2,1,0:T(8,128)} %copy-done, f32[256,256]{1,0:T(8,128)} %get-tuple-element.22.k, f32[256,256]{1,0:T(8,128)} %get-tuple-element.23.k_inv, f32[1,256,1024]{2,1,0:T(8,128)} %front.5), custom_call_target="tpu_custom_call" | custom-call | flops 2147483648 | bytes 4194304 | tf_op jit(solution)/shard_map/finish/pallas_call | solution.py:304
  125.6 1.0 pad_maximum_fusion
  (49 shorter events, 9.8 us)
Async XLA Ops:
  2.6 4.0 %collective-permute-start.6 = (f32[392,128]{1,0:T(8,128)}, f32[392,128]{1,0:T(8,128)S(1)}, u32[]{:S(2)}, u32[]{:S(2)}) collective-permute-start(f32[392,128]{1,0:T(8,128)} %get-tuple-element.21), channel_id=1, source_target_pairs={{0,32},{64,96},{128,160},{192,224}} | collective-permute-start | bytes 602120 | tf_op jit(solution)/shard_map/ppermute | solution.py:333
  3.3 11.9 %collective-permute-start.5 = (f32[72,256]{1,0:T(8,128)}, f32[72,256]{1,0:T(8,128)S(1)}, u32[]{:S(2)}, u32[]{:S(2)}) collective-permute-start(f32[72,256]{1,0:T(8,128)} %get-tuple-element.20), channel_id=1, source_target_pairs={{0,12},{4,28},{8,44},{12,60},{16,13},{20,29},{24,45},{28,61},{32,1... | collective-permute-start | bytes 221192 | tf_op jit(solution)/shard_map/ppermute | solution.py:352
  4.6 10.6 %collective-permute-start.4 = (f32[72,256]{1,0:T(8,128)}, f32[72,256]{1,0:T(8,128)S(1)}, u32[]{:S(2)}, u32[]{:S(2)}) collective-permute-start(f32[72,256]{1,0:T(8,128)} %get-tuple-element.19), channel_id=1, source_target_pairs={{0,8},{4,24},{8,40},{12,56},{16,9},{20,25},{24,41},{28,57},{32,10}... | collective-permute-start | bytes 221192 | tf_op jit(solution)/shard_map/ppermute | solution.py:352
  5.2 9.9 %collective-permute-start.2 = (f32[72,256]{1,0:T(8,128)}, f32[72,256]{1,0:T(8,128)S(1)}, u32[]{:S(2)}, u32[]{:S(2)}) collective-permute-start(f32[72,256]{1,0:T(8,128)} %get-tuple-element.17), channel_id=1, source_target_pairs={{0,0},{4,16},{8,32},{12,48},{16,1},{20,17},{24,33},{28,49},{32,2},... | collective-permute-start | bytes 221192 | tf_op jit(solution)/shard_map/ppermute | solution.py:352
  5.9 9.3 %collective-permute-start.3 = (f32[72,256]{1,0:T(8,128)}, f32[72,256]{1,0:T(8,128)S(1)}, u32[]{:S(2)}, u32[]{:S(2)}) collective-permute-start(f32[72,256]{1,0:T(8,128)} %get-tuple-element.18), channel_id=1, source_target_pairs={{0,4},{4,20},{8,36},{12,52},{16,5},{20,21},{24,37},{28,53},{32,6},... | collective-permute-start | bytes 221192 | tf_op jit(solution)/shard_map/ppermute | solution.py:352
  7.6 20.6 %collective-permute-start.7 = (f32[392,128]{1,0:T(8,128)S(1)}, f32[392,128]{1,0:T(8,128)S(1)}, u32[]{:S(2)}, u32[]{:S(2)}) collective-permute-start(f32[392,128]{1,0:T(8,128)S(1)} %broadcast_select_fusion.2), channel_id=1, source_target_pairs={{0,16},{32,48},{64,80},{96,112},{128,144},{160,176},{192,208},{224... | collective-permute-start | bytes 602120 | tf_op jit(solution)/shard_map/ppermute | solution.py:333
  16.3 67.6 %all-to-all-start = ((f32[16,72,256]{2,1,0:T(8,128)}), f32[16,72,256]{2,1,0:T(8,128)S(1)}, u32[]{:S(2)}, u32[]{:S(2)}) async-start(f32[16,72,256]{2,1,0:T(8,128)} %broadcast_in_dim.2), calls=%async_computation | async-start | bytes 2359296 | tf_op jit(solution)/shard_map/all_to_all | solution.py:359
  28.1 1.6 %copy-start.1 = (f32[256,384]{1,0:T(8,128)S(1)}, f32[256,384]{1,0:T(8,128)}, u32[]{:S(2)}) copy-start(f32[256,384]{1,0:T(8,128)} %get-tuple-element.16) | copy-start | bytes 1179652
  28.2 0.8 collective-permute-start.8
  29.0 2.0 %collective-permute-start.9 = (f32[392,128]{1,0:T(8,128)S(1)}, f32[392,128]{1,0:T(8,128)S(1)}, u32[]{:S(2)}, u32[]{:S(2)}) collective-permute-start(f32[392,128]{1,0:T(8,128)S(1)} %broadcast_select_fusion.4), channel_id=1, source_target_pairs={{0,4},{8,12},{16,20},{24,28},{32,36},{40,44},{48,52},{56,60},{64,6... | collective-permute-start | bytes 602120 | tf_op jit(solution)/shard_map/ppermute | solution.py:333
  29.7 12.8 %collective-permute-start = (f32[256,384]{1,0:T(8,128)S(1)}, f32[256,384]{1,0:T(8,128)S(1)}, u32[]{:S(2)}, u32[]{:S(2)}) collective-permute-start(f32[256,384]{1,0:T(8,128)S(1)} %copy-done.1), channel_id=1, source_target_pairs={{0,2},{4,6},{8,10},{12,14},{16,18},{20,22},{24,26},{28,30},{32,34}... | collective-permute-start | bytes 1179656 | tf_op jit(solution)/shard_map/ppermute | solution.py:339
  31.1 36.9 %collective-permute-start.10 = (f32[392,128]{1,0:T(8,128)S(1)}, f32[392,128]{1,0:T(8,128)S(1)}, u32[]{:S(2)}, u32[]{:S(2)}) collective-permute-start(f32[392,128]{1,0:T(8,128)S(1)} %broadcast_select_fusion.5), channel_id=1, source_target_pairs={{0,2},{4,6},{8,10},{12,14},{16,18},{20,22},{24,26},{28,30},{32,34}... | collective-permute-start | bytes 602120 | tf_op jit(solution)/shard_map/ppermute | solution.py:339
  42.6 26.8 %collective-permute-start.1 = (f32[256,384]{1,0:T(8,128)S(1)}, f32[256,384]{1,0:T(8,128)S(1)}, u32[]{:S(2)}, u32[]{:S(2)}) collective-permute-start(f32[256,384]{1,0:T(8,128)S(1)} %broadcast_select_fusion), channel_id=1, source_target_pairs={{0,1},{2,3},{4,5},{6,7},{8,9},{10,11},{12,13},{14,15},{16,17},{18,... | collective-permute-start | bytes 1179656 | tf_op jit(solution)/shard_map/ppermute | solution.py:344
  68.0 2.4 %collective-permute-start.11 = (f32[392,128]{1,0:T(8,128)S(1)}, f32[392,128]{1,0:T(8,128)S(1)}, u32[]{:S(2)}, u32[]{:S(2)}) collective-permute-start(f32[392,128]{1,0:T(8,128)S(1)} %broadcast_select_fusion.6), channel_id=1, source_target_pairs={{0,1},{2,3},{4,5},{6,7},{8,9},{10,11},{12,13},{14,15},{16,17},{18,... | collective-permute-start | bytes 602120 | tf_op jit(solution)/shard_map/ppermute | solution.py:344
  84.0 1.0 copy-start
  92.4 12.7 %copy-start.2 = (f32[64,1024]{1,0:T(8,128)S(1)}, f32[64,1024]{1,0:T(8,128)}, u32[]{:S(2)}) copy-start(f32[64,1024]{1,0:T(8,128)} %get-tuple-element.26) | copy-start | bytes 786436
  92.4 8.9 %collective-permute-start.16 = (f32[64,1024]{1,0:T(8,128)}, f32[64,1024]{1,0:T(8,128)S(1)}, u32[]{:S(2)}, u32[]{:S(2)}) collective-permute-start(f32[64,1024]{1,0:T(8,128)} %get-tuple-element.29), channel_id=1, source_target_pairs={{0,192},{192,0},{64,128},{128,64},{1,193},{193,1},{65,129},{129,65... | collective-permute-start | bytes 786440 | tf_op jit(solution)/shard_map/ppermute | solution.py:372
  92.9 12.1 %collective-permute-start.12 = (f32[64,1024]{1,0:T(8,128)}, f32[64,1024]{1,0:T(8,128)S(1)}, u32[]{:S(2)}, u32[]{:S(2)}) collective-permute-start(f32[64,1024]{1,0:T(8,128)} %get-tuple-element.27), channel_id=1, source_target_pairs={{0,64},{64,0},{128,192},{192,128},{1,65},{65,1},{129,193},{193,129... | collective-permute-start | bytes 786440 | tf_op jit(solution)/shard_map/ppermute | solution.py:372
  102.3 6.0 %collective-permute-start.17 = (f32[32,1024]{1,0:T(8,128)S(1)}, f32[32,1024]{1,0:T(8,128)S(1)}, u32[]{:S(2)}, u32[]{:S(2)}) collective-permute-start(f32[32,1024]{1,0:T(8,128)S(1)} %constant_dynamic-slice_fusion), channel_id=1, source_target_pairs={{0,64},{64,0},{128,192},{192,128},{1,65},{65,1},{129,193},{193,129... | collective-permute-start | bytes 393224 | tf_op jit(solution)/shard_map/ppermute | solution.py:372
  105.1 5.1 %collective-permute-start.13 = (f32[32,1024]{1,0:T(8,128)S(1)}, f32[32,1024]{1,0:T(8,128)S(1)}, u32[]{:S(2)}, u32[]{:S(2)}) collective-permute-start(f32[32,1024]{1,0:T(8,128)S(1)} %constant_dynamic-slice_fusion.1), channel_id=1, source_target_pairs={{0,192},{192,0},{64,128},{128,64},{1,193},{193,1},{65,129},{129,65... | collective-permute-start | bytes 393224 | tf_op jit(solution)/shard_map/ppermute | solution.py:372
  108.2 5.1 %collective-permute-start.18 = (f32[32,1024]{1,0:T(8,128)S(1)}, f32[32,1024]{1,0:T(8,128)S(1)}, u32[]{:S(2)}, u32[]{:S(2)}) collective-permute-start(f32[32,1024]{1,0:T(8,128)S(1)} %dynamic-slice_add_fusion), channel_id=1, source_target_pairs={{0,64},{64,0},{128,192},{192,128},{1,65},{65,1},{129,193},{193,129... | collective-permute-start | bytes 393224 | tf_op jit(solution)/shard_map/ppermute | solution.py:372
  110.2 6.5 %collective-permute-start.14 = (f32[32,1024]{1,0:T(8,128)S(1)}, f32[32,1024]{1,0:T(8,128)S(1)}, u32[]{:S(2)}, u32[]{:S(2)}) collective-permute-start(f32[32,1024]{1,0:T(8,128)S(1)} %dynamic-slice_add_fusion.1), channel_id=1, source_target_pairs={{0,192},{192,0},{64,128},{128,64},{1,193},{193,1},{65,129},{129,65... | collective-permute-start | bytes 393224 | tf_op jit(solution)/shard_map/ppermute | solution.py:372
  113.3 12.1 %collective-permute-start.19 = (f32[64,1024]{1,0:T(8,128)S(1)}, f32[64,1024]{1,0:T(8,128)S(1)}, u32[]{:S(2)}, u32[]{:S(2)}) collective-permute-start(f32[64,1024]{1,0:T(8,128)S(1)} %maximum_select_fusion.3), channel_id=1, source_target_pairs={{0,192},{192,0},{64,128},{128,64},{1,193},{193,1},{65,129},{129,65... | collective-permute-start | bytes 786440 | tf_op jit(solution)/shard_map/ppermute | solution.py:372
  116.7 8.9 %collective-permute-start.15 = (f32[64,1024]{1,0:T(8,128)S(1)}, f32[64,1024]{1,0:T(8,128)S(1)}, u32[]{:S(2)}, u32[]{:S(2)}) collective-permute-start(f32[64,1024]{1,0:T(8,128)S(1)} %maximum_select_fusion.2), channel_id=1, source_target_pairs={{0,64},{64,0},{128,192},{192,128},{1,65},{65,1},{129,193},{193,129... | collective-permute-start | bytes 786440 | tf_op jit(solution)/shard_map/ppermute | solution.py:372
where the time goes:
time: 127 us
  waiting for transfers between devices  57.9 us (46%)
  starting transfers between devices  32.2 us (25%)
  Pallas kernels  28.4 us (22%)
  other arithmetic  4.84 us (4%)
  local copies, waits for them, and re-layouts  2.22 us (2%)
    ppermute x2, waiting for transfers between devices, spread_far(): got = lax.ppermute(x, PLANE, [(at(q, 0), at(q, 2)) for q in range(ROWS)])  34.2 us
    ppermute x8, waiting for transfers between devices, exchange(): return [lax.ppermute(x, 'leaf', p[turn]) for x, p in zip(xs, pairs)]  16.6 us
    pallas_call x1, Pallas kernels, factor(): pl.pallas_call(factor_body, in_specs=[VMEM], out_specs=[VMEM] * 4, out_sh...  12.9 us
    all_to_all x1, starting transfers between devices, gather_columns(): return lax.all_to_all(copies, 'frow', 0, 0, tiled=True)  11.8 us
    ppermute x8, starting transfers between devices, exchange(): return [lax.ppermute(x, 'leaf', p[turn]) for x, p in zip(xs, pairs)]  9.08 us
    pallas_call x1, Pallas kernels, contribute(): pl.pallas_call(contribute_body, grid=(4,), in_specs=[SMEM, whole(256, 384...  7.35 us
    ppermute x4, waiting for transfers between devices, scatter_columns(): got = lax.ppermute(sent, PLANE, pairs)  6.92 us
    pallas_call x1, Pallas kernels, finish(): pl.pallas_call(finish_body, grid=(4,), in_specs=[whole(256, 384), GATHERE...  6.24 us
  transfers between devices with their start and end apart: 21, of which 8 were waited for; matrix products, arithmetic and copies ran while one was open for 4% of the time, Pallas kernels for 15%

commit v1 on v0

--- a/solution.py
+++ b/solution.py
@@ -102,16 +102,8 @@
     return lax.broadcasted_iota(jnp.int32, shape, 0), lax.broadcasted_iota(jnp.int32, shape, 1)
 
 
-def pack_body(front, parent, pivots, rows, *scattered):
-    leaf = lax.axis_index("leaf")
-    row, col = square()
-    a11 = front[0, :BLOCK, :BLOCK]
-    a22 = front[0, BLOCK:, BLOCK:]
-    pivots[:BLOCK] = jnp.where(col <= row, a11, a22)
-    pivots[BLOCK:PIVOTS] = front[0, BLOCK:, :BLOCK]
-    pivots[PIVOTS : PIVOTS + BLOCK] = parent[:BLOCK]
-    diag = jnp.sum(jnp.where(row == col, a22, 0.0), axis=0, keepdims=True)
-    pivots[PIVOTS + BLOCK :] = jnp.broadcast_to(diag, (8, BLOCK))
+def pack_body(front, parent, pivots, k, kp, rows, *scattered):
+    leaf, r, c = lax.axis_index("leaf"), lax.axis_index("frow"), lax.axis_index("fcol")
     rows[:, :PIVOTS] = front[0]
     rows[:, PIVOTS:] = parent[...]
     for j, out in enumerate(scattered):
@@ -119,6 +111,32 @@
         at_row = pl.multiple_of(64 * leaf + 16 * j, 8)
         out[64:, :BLOCK] = parent[pl.ds(at_row, 8)]
         out[64:, BLOCK:] = parent[pl.ds(at_row + 8, 8)]
+    owner = (r == 0) & (c == 0)
+
+    @pl.when(owner)
+    def _():
+        row, col = square()
+        a11 = front[0, :BLOCK, :BLOCK]
+        ap = parent[:BLOCK]
+        (k1_inv,) = inverse_factors([a11])
+        k21 = mm_t(front[0, BLOCK:, :BLOCK], k1_inv)
+        s22 = front[0, BLOCK:, BLOCK:] - mm_t(k21, k21)
+        k2_inv, parent_inv = inverse_factors([s22, ap])
+        pivots[:BLOCK] = jnp.where(col <= row, k1_inv, k2_inv.T)
+        pivots[BLOCK:PIVOTS] = -mm(k2_inv, mm(k21, k1_inv))
+        pivots[PIVOTS : PIVOTS + BLOCK] = parent_inv
+        diag = jnp.sum(jnp.where(row == col, k2_inv, 0.0), axis=0, keepdims=True)
+        pivots[PIVOTS + BLOCK :] = jnp.broadcast_to(diag, (8, BLOCK))
+        k[:BLOCK, :BLOCK] = jnp.where(col <= row, mm_t(a11, k1_inv), 0.0)
+        k[:BLOCK, BLOCK:] = jnp.zeros((BLOCK, BLOCK), jnp.float32)
+        k[BLOCK:, :BLOCK] = k21
+        k[BLOCK:, BLOCK:] = jnp.where(col <= row, mm_t(s22, k2_inv), 0.0)
+        kp[...] = jnp.where(col <= row, mm_t(ap, parent_inv), 0.0)
+
+    @pl.when(jnp.logical_not(owner))
+    def _():
+        for out in (pivots, k, kp):
+            out[...] = jnp.zeros_like(out)
 
 
 def pack(front, parent):
@@ -129,57 +147,16 @@
             pl.BlockSpec((1, PIVOTS, PIVOTS), lambda i: (0, 0, 0)),
             pl.BlockSpec((PIVOTS, BLOCK), lambda i: (0, 0)),
         ],
-        out_specs=[VMEM] * 6,
-        out_shape=[f32(392, BLOCK), f32(256, 384)] + [f32(72, PIVOTS)] * 4,
+        out_specs=[VMEM] * 8,
+        out_shape=[f32(392, BLOCK), f32(PIVOTS, PIVOTS), f32(BLOCK, BLOCK), f32(256, 384)]
+        + [f32(72, PIVOTS)] * 4,
         name="pack",
     )(front, parent)
 
 
-def factor_body(pivots, k, k_inv, kp, kp_inv):
-    row, col = square()
-    both = pivots[:BLOCK]
-    low = jnp.where(col <= row, both, 0.0)
-    a11 = low + jnp.where(col < row, low, 0.0).T
-    high = jnp.where(col > row, both, 0.0)
-    diag = jnp.broadcast_to(pivots[PIVOTS + BLOCK : PIVOTS + BLOCK + 1], (BLOCK, BLOCK))
-    a22 = high + high.T + jnp.where(row == col, diag, 0.0)
-    a21 = pivots[BLOCK:PIVOTS]
-    ap = pivots[PIVOTS : PIVOTS + BLOCK]
-    (k1_inv,) = inverse_factors([a11])
-    k21 = mm_t(a21, k1_inv)
-    s22 = a22 - mm_t(k21, k21)
-    k2_inv, parent_inv = inverse_factors([s22, ap])
-    zero = jnp.zeros((BLOCK, BLOCK), jnp.float32)
-    k_inv[:BLOCK, :BLOCK] = k1_inv
-    k_inv[:BLOCK, BLOCK:] = zero
-    k_inv[BLOCK:, :BLOCK] = -mm(k2_inv, mm(k21, k1_inv))
-    k_inv[BLOCK:, BLOCK:] = k2_inv
-    k[:BLOCK, :BLOCK] = jnp.where(col <= row, mm_t(a11, k1_inv), 0.0)
-    k[:BLOCK, BLOCK:] = zero
-    k[BLOCK:, :BLOCK] = k21
-    k[BLOCK:, BLOCK:] = jnp.where(col <= row, mm_t(s22, k2_inv), 0.0)
-    kp_inv[...] = parent_inv
-    kp[...] = jnp.where(col <= row, mm_t(ap, parent_inv), 0.0)
-
-
-def factor(pivots):
-    return pl.pallas_call(
-        factor_body,
-        in_specs=[VMEM],
-        out_specs=[VMEM] * 4,
-        out_shape=[f32(PIVOTS, PIVOTS)] * 2 + [f32(BLOCK, BLOCK)] * 2,
-        name="factor",
-    )(pivots)
-
-
-def raw_columns(gathered):
-    return jnp.concatenate([gathered[j, :64] for j in range(4)], axis=0)
-
-
-def contribute_body(
-    maps, rows, gathered, k_inv, kp, kp_inv, front, parent, *rest
+def prepare_body(
+    maps, pivots, kp, rows, front, parent, base, high, low, b_rows, k_inv, kp_inv
 ):
-    outs, (lines_high, lines_low, columns, value) = rest[:4], rest[4:]
     leaf, r, c = lax.axis_index("leaf"), lax.axis_index("frow"), lax.axis_index("fcol")
     i = pl.program_id(0)
     kept_rows = jnp.where(r > 0, 1.0, 0.0)
@@ -187,30 +164,29 @@
 
     @pl.when(i == 0)
     def _():
-        b = mm_t(rows[:, :PIVOTS], k_inv[...]) * kept_rows
+        row, col = square()
+        both = pivots[:BLOCK]
+        diag = jnp.broadcast_to(pivots[PIVOTS + BLOCK : PIVOTS + BLOCK + 1], (BLOCK, BLOCK))
+        k_inv[:BLOCK, :BLOCK] = jnp.where(col <= row, both, 0.0)
+        k_inv[:BLOCK, BLOCK:] = jnp.zeros((BLOCK, BLOCK), jnp.float32)
+        k_inv[BLOCK:, :BLOCK] = pivots[BLOCK:PIVOTS]
+        k_inv[BLOCK:, BLOCK:] = jnp.where(col > row, both, 0.0).T + jnp.where(row == col, diag, 0.0)
+        kp_inv[...] = pivots[PIVOTS : PIVOTS + BLOCK]
+        b = mm_t(rows[:, :PIVOTS], k_inv[...])
+        b_rows[:, :PIVOTS] = b
+        b = b * kept_rows
         bp = mm_t(rows[:, PIVOTS:], kp_inv[...])
+        b_rows[:, PIVOTS:] = bp
         for h in range(2):
             block = slice(h * BLOCK, (h + 1) * BLOCK)
             to = pl.multiple_of((h + turn) % 2 * BLOCK, BLOCK)
-            lines_high[pl.ds(to, BLOCK), :PIVOTS], lines_low[pl.ds(to, BLOCK), :PIVOTS] = halves(b[block])
+            high[pl.ds(to, BLOCK), :PIVOTS], low[pl.ds(to, BLOCK), :PIVOTS] = halves(b[block])
             mine = bp[block] * kept_rows if h == 0 else bp[block]
-            lines_high[block, PIVOTS:], lines_low[block, PIVOTS:] = halves(mine)
-        columns[:, PIVOTS:] = jnp.zeros((256, BLOCK), jnp.float32)
+            high[block, PIVOTS:], low[block, PIVOTS:] = halves(mine)
 
     pair = lax.broadcasted_iota(jnp.int32, (1, BLOCK), 1)
     kept = jnp.where((c > 0) | (i > 0), 1.0, 0.0)
     swap = maps[0, 2 * (4 * c + i)] % 2
-    own = mm_t(raw_columns(gathered), k_inv[...])
-    for h in range(2):
-        to = pl.multiple_of((h + swap) % 2 * BLOCK, BLOCK)
-        columns[pl.ds(to, BLOCK), :PIVOTS] = own[h * BLOCK : (h + 1) * BLOCK] * kept
-    strip = jnp.concatenate(
-        [gathered[j, 64:, half : half + BLOCK] for j in range(4) for half in (0, BLOCK)], axis=0
-    )
-    pivot_strip = (c == 0) & (i == 0) & (leaf < 2)
-    to = pl.multiple_of(64 * leaf, 64)
-    columns[pl.ds(to, 64), PIVOTS:] = mm_t(strip, kp_inv[...]) * jnp.where(pivot_strip, 0.0, 1.0)
-    update = product_t((lines_high[...], lines_low[...]), halves(columns[...]))
     for h in range(2):
         from_row = pl.multiple_of((h + turn) % 2 * BLOCK, BLOCK)
         block = slice(h * BLOCK, (h + 1) * BLOCK)
@@ -222,16 +198,70 @@
             theirs = parent[block, strips]
             if h == 0:
                 theirs = theirs * kept_rows
-            value[block, strips] = child + jnp.where(mine, theirs, 0.0) - update[block, strips]
+            base[block, strips] = child + jnp.where(mine, theirs, 0.0)
 
     @pl.when((c == 0) & (i == 0))
     def _():
         mine = pair // 64 == leaf
-        bp = mm_t(rows[:, PIVOTS:], kp_inv[...])
-        top = jnp.where(r == 0, kp[...], bp[:BLOCK])
-        value[:BLOCK, :BLOCK] = jnp.where(mine, top, 0.0)
-        value[BLOCK:, :BLOCK] = jnp.where(mine, bp[BLOCK:], 0.0)
-
+        top = jnp.where(r == 0, kp[...], b_rows[:BLOCK, PIVOTS:])
+        base[:BLOCK, :BLOCK] = jnp.where(mine, top, 0.0)
+        base[BLOCK:, :BLOCK] = jnp.where(mine, b_rows[BLOCK:, PIVOTS:], 0.0)
+
+
+def whole(*shape):
+    return pl.BlockSpec(shape, lambda i: (0,) * len(shape))
+
+
+GATHERED = pl.BlockSpec((4, 72, PIVOTS), lambda i: (i, 0, 0))
+FRONT = pl.BlockSpec((1, 256, 256), lambda i: (0, 0, i))
+PARENT = pl.BlockSpec((256, 256), lambda i: (0, i))
+
+
+def prepare(maps, pivots, kp, rows, front, parent):
+    half = jax.ShapeDtypeStruct((256, 384), jnp.bfloat16)
+    return pl.pallas_call(
+        prepare_body,
+        grid=(4,),
+        in_specs=[SMEM, whole(392, BLOCK), whole(BLOCK, BLOCK), whole(256, 384), FRONT, PARENT],
+        out_specs=[
+            PARENT,
+            whole(256, 384),
+            whole(256, 384),
+            whole(256, 384),
+            whole(PIVOTS, PIVOTS),
+            whole(BLOCK, BLOCK),
+        ],
+        out_shape=[f32(256, 1024), half, half, f32(256, 384), f32(PIVOTS, PIVOTS), f32(BLOCK, BLOCK)],
+        name="prepare",
+    )(maps, pivots, kp, rows, front, parent)
+
+
+def raw_columns(gathered):
+    return jnp.concatenate([gathered[j, :64] for j in range(4)], axis=0)
+
+
+def contribute_body(maps, gathered, k_inv, kp_inv, base, high, low, *rest):
+    outs, (columns, value) = rest[:4], rest[4:]
+    leaf, c = lax.axis_index("leaf"), lax.axis_index("fcol")
+    i = pl.program_id(0)
+
+    @pl.when(i == 0)
+    def _():
+        columns[:, PIVOTS:] = jnp.zeros((256, BLOCK), jnp.float32)
+
+    kept = jnp.where((c > 0) | (i > 0), 1.0, 0.0)
+    swap = maps[0, 2 * (4 * c + i)] % 2
+    own = mm_t(raw_columns(gathered), k_inv[...])
+    for h in range(2):
+        to = pl.multiple_of((h + swap) % 2 * BLOCK, BLOCK)
+        columns[pl.ds(to, BLOCK), :PIVOTS] = own[h * BLOCK : (h + 1) * BLOCK] * kept
+    strip = jnp.concatenate(
+        [gathered[j, 64:, half : half + BLOCK] for j in range(4) for half in (0, BLOCK)], axis=0
+    )
+    pivot_strip = (c == 0) & (i == 0) & (leaf < 2)
+    to = pl.multiple_of(64 * leaf, 64)
+    columns[pl.ds(to, 64), PIVOTS:] = mm_t(strip, kp_inv[...]) * jnp.where(pivot_strip, 0.0, 1.0)
+    value[...] = base[...] - product_t((high[...], low[...]), halves(columns[...]))
     for half, bit in enumerate(first_bits(leaf)):
         for out, at_row in ((outs[2 * half], 1 - bit), (outs[2 * half + 1], bit)):
             out[...] = value[pl.ds(pl.multiple_of(BLOCK * half + 64 * at_row, 64), 64)]
@@ -241,50 +271,33 @@
     return jnp.where((leaf == 1) | (leaf == 2), 1, 0), leaf // 2
 
 
-def whole(*shape):
-    return pl.BlockSpec(shape, lambda i: (0,) * len(shape))
-
-
-GATHERED = pl.BlockSpec((4, 72, PIVOTS), lambda i: (i, 0, 0))
-FRONT = pl.BlockSpec((1, 256, 256), lambda i: (0, 0, i))
-PARENT = pl.BlockSpec((256, 256), lambda i: (0, i))
-
-
-def contribute(maps, rows, gathered, k_inv, kp, kp_inv, front, parent):
+def contribute(maps, gathered, k_inv, kp_inv, base, high, low):
     return pl.pallas_call(
         contribute_body,
         grid=(4,),
         in_specs=[
             SMEM,
-            whole(256, 384),
             GATHERED,
             whole(PIVOTS, PIVOTS),
             whole(BLOCK, BLOCK),
-            whole(BLOCK, BLOCK),
-            FRONT,
             PARENT,
+            whole(256, 384),
+            whole(256, 384),
         ],
         out_specs=[pl.BlockSpec((64, 256), lambda i: (0, i))] * 4,
         out_shape=[f32(64, 1024)] * 4,
-        scratch_shapes=[
-            pltpu.VMEM((256, 384), jnp.bfloat16),
-            pltpu.VMEM((256, 384), jnp.bfloat16),
-            pltpu.VMEM((256, 384), jnp.float32),
-            pltpu.VMEM((256, 256), jnp.float32),
-        ],
+        scratch_shapes=[pltpu.VMEM((256, 384), jnp.float32), pltpu.VMEM((256, 256), jnp.float32)],
         name="contribute",
-    )(maps, rows, gathered, k_inv, kp, kp_inv, front, parent)
-
-
-def finish_body(rows, gathered, k, k_inv, front, out, b_rows, high, low):
+    )(maps, gathered, k_inv, kp_inv, base, high, low)
+
+
+def finish_body(b_rows, gathered, k, k_inv, front, out, high, low):
     r, c = lax.axis_index("frow"), lax.axis_index("fcol")
     i = pl.program_id(0)
 
     @pl.when(i == 0)
     def _():
-        b = mm_t(rows[:, :PIVOTS], k_inv[...])
-        b_rows[...] = b
-        high[...], low[...] = halves(b)
+        high[...], low[...] = halves(b_rows[:, :PIVOTS])
 
     @pl.when(r == 0)
     def _():
@@ -297,10 +310,10 @@
 
     @pl.when((c == 0) & (i == 0))
     def _():
-        out[0] = jnp.where(r == 0, k[...], b_rows[...])
-
-
-def finish(rows, gathered, k, k_inv, front):
+        out[0] = jnp.where(r == 0, k[...], b_rows[:, :PIVOTS])
+
+
+def finish(b_rows, gathered, k, k_inv, front):
     return pl.pallas_call(
         finish_body,
         grid=(4,),
@@ -314,13 +327,12 @@
         out_specs=FRONT,
         out_shape=f32(1, 256, 1024),
         scratch_shapes=[
-            pltpu.VMEM((256, 256), jnp.float32),
             pltpu.VMEM((256, 256), jnp.bfloat16),
             pltpu.VMEM((256, 256), jnp.bfloat16),
         ],
         cost_estimate=pl.CostEstimate(flops=1 << 31, bytes_accessed=4 << 20, transcendentals=0),
         name="finish",
-    )(rows, gathered, k, k_inv, front)
+    )(b_rows, gathered, k, k_inv, front)
 
 
 def at(r, c):
@@ -369,7 +381,10 @@
     second = (leaf // 2, leaf % 2)
 
     def exchange(xs, turn):
-        return [lax.ppermute(x, "leaf", p[turn]) for x, p in zip(xs, pairs)]
+        got = []
+        for x, p in zip(xs, pairs):
+            got.append(lax.ppermute(x, "leaf", p[turn]))
+        return got
 
     def ordered(bit, mine, got):
         return jnp.where(bit == 0, jnp.concatenate([mine, got]), jnp.concatenate([got, mine]))
@@ -390,7 +405,7 @@
     leaf = lax.axis_index("leaf")
     r = lax.axis_index("frow")
     c = lax.axis_index("fcol")
-    pivots, rows, *scattered = pack(child_fronts, parent_front)
+    pivots, k, kp, rows, *scattered = pack(child_fronts, parent_front)
     pivots = spread_rows(pivots, r, (8, 4, 2))
     rows = spread_far(rows, c)
     piece = scatter_columns(scattered)
@@ -399,12 +414,13 @@
     pivots = spread_far(pivots, c)
     pivots = spread_core(pivots, c)
     rows = spread_core(rows, c)
-    k, k_inv, kp, kp_inv = factor(pivots)
-    parts = contribute(
-        block_maps, rows, gathered, k_inv, kp, kp_inv, child_fronts, parent_front
-    )
+    base, high, low, b_rows, k_inv, kp_inv = prepare(
+        block_maps, pivots, kp, rows, child_fronts, parent_front
+    )
+    parts = contribute(block_maps, gathered, k_inv, kp_inv, base, high, low)
     parent_done = sum_over_leaf(parts, leaf)
-    return finish(rows, gathered, k, k_inv, child_fronts), parent_done
+    finished = finish(b_rows, gathered, k, k_inv, child_fronts)
+    return finished, parent_done
 
 
 def solution(mesh):

time: 127 us -> 117 us (0.921)
  the two profiles are of different devices: /device:TPU:54 before, /device:TPU:46 now
where the time goes in v1:
time: 117 us; the launch traced here: 116 us
  waiting for transfers between devices  52.3 us (45%)
  starting transfers between devices  36.7 us (31%)
  Pallas kernels  19.3 us (16%)
  other arithmetic  4.83 us (4%)
  local copies, waits for them, and re-layouts  2.21 us (2%)
    ppermute x2, waiting for transfers between devices, spread_far(): got = lax.ppermute(x, PLANE, [(at(q, 0), at(q, 2)) for q in range(ROWS)])  33.4 us
    ppermute x8, starting transfers between devices, exchange(): got.append(lax.ppermute(x, 'leaf', p[turn]))  15.2 us
    ppermute x8, waiting for transfers between devices, exchange(): got.append(lax.ppermute(x, 'leaf', p[turn]))  10.4 us
    all_to_all x1, starting transfers between devices, gather_columns(): return lax.all_to_all(copies, 'frow', 0, 0, tiled=True)  10 us
    ppermute x4, waiting for transfers between devices, scatter_columns(): got = lax.ppermute(sent, PLANE, pairs)  8.37 us
    pallas_call x1, Pallas kernels, contribute(): pl.pallas_call(contribute_body, grid=(4,), in_specs=[SMEM, GATHERED, whol...  6.54 us
    pallas_call x1, Pallas kernels, finish(): pl.pallas_call(finish_body, grid=(4,), in_specs=[whole(256, 384), GATHERE...  5.87 us
    pallas_call x1, Pallas kernels, prepare(): pl.pallas_call(prepare_body, grid=(4,), in_specs=[SMEM, whole(392, BLOCK)...  4.81 us
  transfers between devices with their start and end apart: 21, of which 8 were waited for; matrix products, arithmetic and copies ran while one was open for 4% of the time, Pallas kernels for 9%

profile of v1, /device:TPU:46, one launch (start us, length us, event | category | flops | bytes accessed | tf_op | source)
XLA Modules:
  0.0 116.4 jit_solution(15358439089788995689)
XLA Ops:
  0.6 2.1 %pack.1 = (f32[392,128]{1,0:T(8,128)}, f32[256,256]{1,0:T(8,128)}, f32[128,128]{1,0:T(8,128)}, f32[256,384]{1,0:T(8,128)}, f32[72,256]{1,0:T(8,128)}, /*index=5*...) custom-call(f32[1,256,1024]{2,1,0:T(8,128)} %front.5, f32[256,1024]{1,0:T(8,128)} %parent.3), custom_call_target="tpu_custom_call" | custom-call | tf_op jit(solution)/shard_map/pack/pallas_call | solution.py:143
  4.0 1.3 %collective-permute-start.11 = (f32[72,256]{1,0:T(8,128)}, f32[72,256]{1,0:T(8,128)S(1)}, u32[]{:S(2)}, u32[]{:S(2)}) collective-permute-start(f32[72,256]{1,0:T(8,128)} %get-tuple-element.27), channel_id=1, source_target_pairs={{0,12},{4,28},{8,44},{12,60},{16,13},{20,29},{24,45},{28,61},{32,1... | collective-permute-start | bytes 221192 | tf_op jit(solution)/shard_map/ppermute | solution.py:364
  8.4 8.4 %collective-permute-done.11 = f32[72,256]{1,0:T(8,128)S(1)} collective-permute-done((f32[72,256]{1,0:T(8,128)}, f32[72,256]{1,0:T(8,128)S(1)}, u32[]{:S(2)}, u32[]{:S(2)}) %collective-permute-start.11) | collective-permute-done | bytes 73760 | tf_op jit(solution)/shard_map/ppermute | solution.py:364
  17.9 10.0 %all-to-all-start = ((f32[16,72,256]{2,1,0:T(8,128)}), f32[16,72,256]{2,1,0:T(8,128)S(1)}, u32[]{:S(2)}, u32[]{:S(2)}) async-start(f32[16,72,256]{2,1,0:T(8,128)} %broadcast_in_dim.2), calls=%async_computation | async-start | bytes 2359296 | tf_op jit(solution)/shard_map/all_to_all | solution.py:371
  29.5 1.3 %collective-permute-start.6 = (f32[256,384]{1,0:T(8,128)S(1)}, f32[256,384]{1,0:T(8,128)S(1)}, u32[]{:S(2)}, u32[]{:S(2)}) collective-permute-start(f32[256,384]{1,0:T(8,128)S(1)} %copy-done.1), channel_id=1, source_target_pairs={{0,2},{4,6},{8,10},{12,14},{16,18},{20,22},{24,26},{28,30},{32,34}... | collective-permute-start | bytes 1179656 | tf_op jit(solution)/shard_map/ppermute | solution.py:351
  32.2 12.8 %collective-permute-done.6 = f32[256,384]{1,0:T(8,128)S(1)} collective-permute-done((f32[256,384]{1,0:T(8,128)S(1)}, f32[256,384]{1,0:T(8,128)S(1)}, u32[]{:S(2)}, u32[]{:S(2)}) %collective-permute-start.6) | collective-permute-done | bytes 393248 | tf_op jit(solution)/shard_map/ppermute | solution.py:351
  45.0 1.3 %collective-permute-start.7 = (f32[256,384]{1,0:T(8,128)S(1)}, f32[256,384]{1,0:T(8,128)S(1)}, u32[]{:S(2)}, u32[]{:S(2)}) collective-permute-start(f32[256,384]{1,0:T(8,128)S(1)} %broadcast_select_fusion), channel_id=1, source_target_pairs={{0,1},{2,3},{4,5},{6,7},{8,9},{10,11},{12,13},{14,15},{16,17},{18,... | collective-permute-start | bytes 1179656 | tf_op jit(solution)/shard_map/ppermute | solution.py:356
  46.4 20.6 %collective-permute-done.4 = f32[392,128]{1,0:T(8,128)S(1)} collective-permute-done((f32[392,128]{1,0:T(8,128)S(1)}, f32[392,128]{1,0:T(8,128)S(1)}, u32[]{:S(2)}, u32[]{:S(2)}) %collective-permute-start.4) | collective-permute-done | bytes 200736 | tf_op jit(solution)/shard_map/ppermute | solution.py:351
  67.0 1.5 %collective-permute-start.5 = (f32[392,128]{1,0:T(8,128)S(1)}, f32[392,128]{1,0:T(8,128)S(1)}, u32[]{:S(2)}, u32[]{:S(2)}) collective-permute-start(f32[392,128]{1,0:T(8,128)S(1)} %broadcast_select_fusion.6), channel_id=1, source_target_pairs={{0,1},{2,3},{4,5},{6,7},{8,9},{10,11},{12,13},{14,15},{16,17},{18,... | collective-permute-start | bytes 602120 | tf_op jit(solution)/shard_map/ppermute | solution.py:356
  70.1 4.8 %prepare.1 = (f32[256,1024]{1,0:T(8,128)}, bf16[256,384]{1,0:T(8,128)(2,1)}, bf16[256,384]{1,0:T(8,128)(2,1)}, f32[256,384]{1,0:T(8,128)}, f32[256,256]{1,0:T(8,128)}, /*index=5*/f32[128,128]{1,0:T(8,128)}) custom-call(s32[1,32]{1,0:T(1,128)} %maps.3, f32[392,128]{1,0:T(8,128)} %broadcast_select_fusion.7.pivots, f32[128,128]{1,0:T(8,128)} %get-tuple-element.21.kp, ...), custom_call_target="tpu_custom_call" | custom-call | tf_op jit(solution)/shard_map/prepare/pallas_call | solution.py:222
  76.0 6.5 %contribute.1 = (f32[64,1024]{1,0:T(8,128)}, f32[64,1024]{1,0:T(8,128)}, f32[64,1024]{1,0:T(8,128)}, f32[64,1024]{1,0:T(8,128)}) custom-call(s32[1,32]{1,0:T(1,128)} %maps.3, f32[16,72,256]{2,1,0:T(8,128)} %copy-done, f32[256,256]{1,0:T(8,128)} %get-tuple-element.29.k_inv, f32[128,128]{1,0:T(8,128)} %get-tuple-element.30.kp_inv, ...), custom_call_target="tpu_custom_call" | custom-call | tf_op jit(solution)/shard_map/contribute/pallas_call | solution.py:275
  82.5 1.7 %collective-permute-start.16 = (f32[64,1024]{1,0:T(8,128)}, f32[64,1024]{1,0:T(8,128)S(1)}, u32[]{:S(2)}, u32[]{:S(2)}) collective-permute-start(f32[64,1024]{1,0:T(8,128)} %get-tuple-element.37), channel_id=1, source_target_pairs={{0,192},{192,0},{64,128},{128,64},{1,193},{193,1},{65,129},{129,65... | collective-permute-start | bytes 786440 | tf_op jit(solution)/shard_map/ppermute | solution.py:386
  84.2 1.9 %collective-permute-start.12 = (f32[64,1024]{1,0:T(8,128)}, f32[64,1024]{1,0:T(8,128)S(1)}, u32[]{:S(2)}, u32[]{:S(2)}) collective-permute-start(f32[64,1024]{1,0:T(8,128)} %get-tuple-element.35), channel_id=1, source_target_pairs={{0,64},{64,0},{128,192},{192,128},{1,65},{65,1},{129,193},{193,129... | collective-permute-start | bytes 786440 | tf_op jit(solution)/shard_map/ppermute | solution.py:386
  86.1 5.3 %collective-permute-done.16 = f32[64,1024]{1,0:T(8,128)S(1)} collective-permute-done((f32[64,1024]{1,0:T(8,128)}, f32[64,1024]{1,0:T(8,128)S(1)}, u32[]{:S(2)}, u32[]{:S(2)}) %collective-permute-start.16) | collective-permute-done | bytes 262176 | tf_op jit(solution)/shard_map/ppermute | solution.py:386
  92.4 2.7 %collective-permute-start.17 = (f32[32,1024]{1,0:T(8,128)S(1)}, f32[32,1024]{1,0:T(8,128)S(1)}, u32[]{:S(2)}, u32[]{:S(2)}) collective-permute-start(f32[32,1024]{1,0:T(8,128)S(1)} %constant_dynamic-slice_fusion), channel_id=1, source_target_pairs={{0,64},{64,0},{128,192},{192,128},{1,65},{65,1},{129,193},{193,129... | collective-permute-start | bytes 393224 | tf_op jit(solution)/shard_map/ppermute | solution.py:386
  95.2 1.5 %collective-permute-start.13 = (f32[32,1024]{1,0:T(8,128)S(1)}, f32[32,1024]{1,0:T(8,128)S(1)}, u32[]{:S(2)}, u32[]{:S(2)}) collective-permute-start(f32[32,1024]{1,0:T(8,128)S(1)} %constant_dynamic-slice_fusion.1), channel_id=1, source_target_pairs={{0,192},{192,0},{64,128},{128,64},{1,193},{193,1},{65,129},{129,65... | collective-permute-start | bytes 393224 | tf_op jit(solution)/shard_map/ppermute | solution.py:386
  96.7 1.6 %collective-permute-done.17 = f32[32,1024]{1,0:T(8,128)S(1)} collective-permute-done((f32[32,1024]{1,0:T(8,128)S(1)}, f32[32,1024]{1,0:T(8,128)S(1)}, u32[]{:S(2)}, u32[]{:S(2)}) %collective-permute-start.17) | collective-permute-done | bytes 131104 | tf_op jit(solution)/shard_map/ppermute | solution.py:386
  98.3 1.9 %collective-permute-start.18 = (f32[32,1024]{1,0:T(8,128)S(1)}, f32[32,1024]{1,0:T(8,128)S(1)}, u32[]{:S(2)}, u32[]{:S(2)}) collective-permute-start(f32[32,1024]{1,0:T(8,128)S(1)} %dynamic-slice_add_fusion), channel_id=1, source_target_pairs={{0,64},{64,0},{128,192},{192,128},{1,65},{65,1},{129,193},{193,129... | collective-permute-start | bytes 393224 | tf_op jit(solution)/shard_map/ppermute | solution.py:386
  100.3 1.5 %collective-permute-start.14 = (f32[32,1024]{1,0:T(8,128)S(1)}, f32[32,1024]{1,0:T(8,128)S(1)}, u32[]{:S(2)}, u32[]{:S(2)}) collective-permute-start(f32[32,1024]{1,0:T(8,128)S(1)} %dynamic-slice_add_fusion.1), channel_id=1, source_target_pairs={{0,192},{192,0},{64,128},{128,64},{1,193},{193,1},{65,129},{129,65... | collective-permute-start | bytes 393224 | tf_op jit(solution)/shard_map/ppermute | solution.py:386
  101.8 1.6 %collective-permute-done.18 = f32[32,1024]{1,0:T(8,128)S(1)} collective-permute-done((f32[32,1024]{1,0:T(8,128)S(1)}, f32[32,1024]{1,0:T(8,128)S(1)}, u32[]{:S(2)}, u32[]{:S(2)}) %collective-permute-start.18) | collective-permute-done | bytes 131104 | tf_op jit(solution)/shard_map/ppermute | solution.py:386
  103.4 1.5 %collective-permute-start.19 = (f32[64,1024]{1,0:T(8,128)S(1)}, f32[64,1024]{1,0:T(8,128)S(1)}, u32[]{:S(2)}, u32[]{:S(2)}) collective-permute-start(f32[64,1024]{1,0:T(8,128)S(1)} %maximum_select_fusion.3), channel_id=1, source_target_pairs={{0,192},{192,0},{64,128},{128,64},{1,193},{193,1},{65,129},{129,65... | collective-permute-start | bytes 786440 | tf_op jit(solution)/shard_map/ppermute | solution.py:386
  104.9 1.8 %collective-permute-done.14 = f32[32,1024]{1,0:T(8,128)S(1)} collective-permute-done((f32[32,1024]{1,0:T(8,128)S(1)}, f32[32,1024]{1,0:T(8,128)S(1)}, u32[]{:S(2)}, u32[]{:S(2)}) %collective-permute-start.14) | collective-permute-done | bytes 131104 | tf_op jit(solution)/shard_map/ppermute | solution.py:386
  106.8 2.6 %collective-permute-start.15 = (f32[64,1024]{1,0:T(8,128)S(1)}, f32[64,1024]{1,0:T(8,128)S(1)}, u32[]{:S(2)}, u32[]{:S(2)}) collective-permute-start(f32[64,1024]{1,0:T(8,128)S(1)} %maximum_select_fusion.2), channel_id=1, source_target_pairs={{0,64},{64,0},{128,192},{192,128},{1,65},{65,1},{129,193},{193,129... | collective-permute-start | bytes 786440 | tf_op jit(solution)/shard_map/ppermute | solution.py:386
  109.3 5.9 %finish.1 = f32[1,256,1024]{2,1,0:T(8,128)} custom-call(f32[256,384]{1,0:T(8,128)} %get-tuple-element.23.b_rows, f32[16,72,256]{2,1,0:T(8,128)} %copy-done, f32[256,256]{1,0:T(8,128)} %get-tuple-element.28.k, f32[256,256]{1,0:T(8,128)} %get-tuple-element.29.k_inv, f32[1,256,1024]{2,1,0:T(8,128)} %front.5), custom_call_target="tpu_custom_call" | custom-call | flops 2147483648 | bytes 4194304 | tf_op jit(solution)/shard_map/finish/pallas_call | solution.py:317
  (49 shorter events, 13.3 us)
Async XLA Ops:
  2.7 4.0 %collective-permute-start = (f32[392,128]{1,0:T(8,128)}, f32[392,128]{1,0:T(8,128)S(1)}, u32[]{:S(2)}, u32[]{:S(2)}) collective-permute-start(f32[392,128]{1,0:T(8,128)} %get-tuple-element.20), channel_id=1, source_target_pairs={{0,32},{64,96},{128,160},{192,224}} | collective-permute-start | bytes 602120 | tf_op jit(solution)/shard_map/ppermute | solution.py:345
  3.4 5.0 %collective-permute-start.10 = (f32[72,256]{1,0:T(8,128)}, f32[72,256]{1,0:T(8,128)S(1)}, u32[]{:S(2)}, u32[]{:S(2)}) collective-permute-start(f32[72,256]{1,0:T(8,128)} %get-tuple-element.26), channel_id=1, source_target_pairs={{0,8},{4,24},{8,40},{12,56},{16,9},{20,25},{24,41},{28,57},{32,10}... | collective-permute-start | bytes 221192 | tf_op jit(solution)/shard_map/ppermute | solution.py:364
  4.0 12.7 %collective-permute-start.11 = (f32[72,256]{1,0:T(8,128)}, f32[72,256]{1,0:T(8,128)S(1)}, u32[]{:S(2)}, u32[]{:S(2)}) collective-permute-start(f32[72,256]{1,0:T(8,128)} %get-tuple-element.27), channel_id=1, source_target_pairs={{0,12},{4,28},{8,44},{12,60},{16,13},{20,29},{24,45},{28,61},{32,1... | collective-permute-start | bytes 221192 | tf_op jit(solution)/shard_map/ppermute | solution.py:364
  5.3 11.4 %collective-permute-start.8 = (f32[72,256]{1,0:T(8,128)}, f32[72,256]{1,0:T(8,128)S(1)}, u32[]{:S(2)}, u32[]{:S(2)}) collective-permute-start(f32[72,256]{1,0:T(8,128)} %get-tuple-element.24), channel_id=1, source_target_pairs={{0,0},{4,16},{8,32},{12,48},{16,1},{20,17},{24,33},{28,49},{32,2},... | collective-permute-start | bytes 221192 | tf_op jit(solution)/shard_map/ppermute | solution.py:364
  6.0 10.7 %collective-permute-start.9 = (f32[72,256]{1,0:T(8,128)}, f32[72,256]{1,0:T(8,128)S(1)}, u32[]{:S(2)}, u32[]{:S(2)}) collective-permute-start(f32[72,256]{1,0:T(8,128)} %get-tuple-element.25), channel_id=1, source_target_pairs={{0,4},{4,20},{8,36},{12,52},{16,5},{20,21},{24,37},{28,53},{32,6},... | collective-permute-start | bytes 221192 | tf_op jit(solution)/shard_map/ppermute | solution.py:364
  7.7 20.2 %collective-permute-start.1 = (f32[392,128]{1,0:T(8,128)S(1)}, f32[392,128]{1,0:T(8,128)S(1)}, u32[]{:S(2)}, u32[]{:S(2)}) collective-permute-start(f32[392,128]{1,0:T(8,128)S(1)} %broadcast_select_fusion.2), channel_id=1, source_target_pairs={{0,16},{32,48},{64,80},{96,112},{128,144},{160,176},{192,208},{224... | collective-permute-start | bytes 602120 | tf_op jit(solution)/shard_map/ppermute | solution.py:345
  17.9 57.0 %all-to-all-start = ((f32[16,72,256]{2,1,0:T(8,128)}), f32[16,72,256]{2,1,0:T(8,128)S(1)}, u32[]{:S(2)}, u32[]{:S(2)}) async-start(f32[16,72,256]{2,1,0:T(8,128)} %broadcast_in_dim.2), calls=%async_computation | async-start | bytes 2359296 | tf_op jit(solution)/shard_map/all_to_all | solution.py:371
  27.9 1.6 %copy-start.1 = (f32[256,384]{1,0:T(8,128)S(1)}, f32[256,384]{1,0:T(8,128)}, u32[]{:S(2)}) copy-start(f32[256,384]{1,0:T(8,128)} %get-tuple-element.22) | copy-start | bytes 1179652
  28.0 0.8 collective-permute-start.2
  28.8 2.0 %collective-permute-start.3 = (f32[392,128]{1,0:T(8,128)S(1)}, f32[392,128]{1,0:T(8,128)S(1)}, u32[]{:S(2)}, u32[]{:S(2)}) collective-permute-start(f32[392,128]{1,0:T(8,128)S(1)} %broadcast_select_fusion.4), channel_id=1, source_target_pairs={{0,4},{8,12},{16,20},{24,28},{32,36},{40,44},{48,52},{56,60},{64,6... | collective-permute-start | bytes 602120 | tf_op jit(solution)/shard_map/ppermute | solution.py:345
  29.5 15.5 %collective-permute-start.6 = (f32[256,384]{1,0:T(8,128)S(1)}, f32[256,384]{1,0:T(8,128)S(1)}, u32[]{:S(2)}, u32[]{:S(2)}) collective-permute-start(f32[256,384]{1,0:T(8,128)S(1)} %copy-done.1), channel_id=1, source_target_pairs={{0,2},{4,6},{8,10},{12,14},{16,18},{20,22},{24,26},{28,30},{32,34}... | collective-permute-start | bytes 1179656 | tf_op jit(solution)/shard_map/ppermute | solution.py:351
  30.9 36.1 %collective-permute-start.4 = (f32[392,128]{1,0:T(8,128)S(1)}, f32[392,128]{1,0:T(8,128)S(1)}, u32[]{:S(2)}, u32[]{:S(2)}) collective-permute-start(f32[392,128]{1,0:T(8,128)S(1)} %broadcast_select_fusion.5), channel_id=1, source_target_pairs={{0,2},{4,6},{8,10},{12,14},{16,18},{20,22},{24,26},{28,30},{32,34}... | collective-permute-start | bytes 602120 | tf_op jit(solution)/shard_map/ppermute | solution.py:351
  45.0 23.5 %collective-permute-start.7 = (f32[256,384]{1,0:T(8,128)S(1)}, f32[256,384]{1,0:T(8,128)S(1)}, u32[]{:S(2)}, u32[]{:S(2)}) collective-permute-start(f32[256,384]{1,0:T(8,128)S(1)} %broadcast_select_fusion), channel_id=1, source_target_pairs={{0,1},{2,3},{4,5},{6,7},{8,9},{10,11},{12,13},{14,15},{16,17},{18,... | collective-permute-start | bytes 1179656 | tf_op jit(solution)/shard_map/ppermute | solution.py:356
  67.0 2.4 %collective-permute-start.5 = (f32[392,128]{1,0:T(8,128)S(1)}, f32[392,128]{1,0:T(8,128)S(1)}, u32[]{:S(2)}, u32[]{:S(2)}) collective-permute-start(f32[392,128]{1,0:T(8,128)S(1)} %broadcast_select_fusion.6), channel_id=1, source_target_pairs={{0,1},{2,3},{4,5},{6,7},{8,9},{10,11},{12,13},{14,15},{16,17},{18,... | collective-permute-start | bytes 602120 | tf_op jit(solution)/shard_map/ppermute | solution.py:356
  74.9 1.0 copy-start
  82.5 12.6 %copy-start.2 = (f32[64,1024]{1,0:T(8,128)S(1)}, f32[64,1024]{1,0:T(8,128)}, u32[]{:S(2)}) copy-start(f32[64,1024]{1,0:T(8,128)} %get-tuple-element.34) | copy-start | bytes 786436
  82.5 8.9 %collective-permute-start.16 = (f32[64,1024]{1,0:T(8,128)}, f32[64,1024]{1,0:T(8,128)S(1)}, u32[]{:S(2)}, u32[]{:S(2)}) collective-permute-start(f32[64,1024]{1,0:T(8,128)} %get-tuple-element.37), channel_id=1, source_target_pairs={{0,192},{192,0},{64,128},{128,64},{1,193},{193,1},{65,129},{129,65... | collective-permute-start | bytes 786440 | tf_op jit(solution)/shard_map/ppermute | solution.py:386
  84.2 11.0 %collective-permute-start.12 = (f32[64,1024]{1,0:T(8,128)}, f32[64,1024]{1,0:T(8,128)S(1)}, u32[]{:S(2)}, u32[]{:S(2)}) collective-permute-start(f32[64,1024]{1,0:T(8,128)} %get-tuple-element.35), channel_id=1, source_target_pairs={{0,64},{64,0},{128,192},{192,128},{1,65},{65,1},{129,193},{193,129... | collective-permute-start | bytes 786440 | tf_op jit(solution)/shard_map/ppermute | solution.py:386
  92.4 5.9 %collective-permute-start.17 = (f32[32,1024]{1,0:T(8,128)S(1)}, f32[32,1024]{1,0:T(8,128)S(1)}, u32[]{:S(2)}, u32[]{:S(2)}) collective-permute-start(f32[32,1024]{1,0:T(8,128)S(1)} %constant_dynamic-slice_fusion), channel_id=1, source_target_pairs={{0,64},{64,0},{128,192},{192,128},{1,65},{65,1},{129,193},{193,129... | collective-permute-start | bytes 393224 | tf_op jit(solution)/shard_map/ppermute | solution.py:386
  95.2 5.1 %collective-permute-start.13 = (f32[32,1024]{1,0:T(8,128)S(1)}, f32[32,1024]{1,0:T(8,128)S(1)}, u32[]{:S(2)}, u32[]{:S(2)}) collective-permute-start(f32[32,1024]{1,0:T(8,128)S(1)} %constant_dynamic-slice_fusion.1), channel_id=1, source_target_pairs={{0,192},{192,0},{64,128},{128,64},{1,193},{193,1},{65,129},{129,65... | collective-permute-start | bytes 393224 | tf_op jit(solution)/shard_map/ppermute | solution.py:386
  98.3 5.1 %collective-permute-start.18 = (f32[32,1024]{1,0:T(8,128)S(1)}, f32[32,1024]{1,0:T(8,128)S(1)}, u32[]{:S(2)}, u32[]{:S(2)}) collective-permute-start(f32[32,1024]{1,0:T(8,128)S(1)} %dynamic-slice_add_fusion), channel_id=1, source_target_pairs={{0,64},{64,0},{128,192},{192,128},{1,65},{65,1},{129,193},{193,129... | collective-permute-start | bytes 393224 | tf_op jit(solution)/shard_map/ppermute | solution.py:386
  100.3 6.5 %collective-permute-start.14 = (f32[32,1024]{1,0:T(8,128)S(1)}, f32[32,1024]{1,0:T(8,128)S(1)}, u32[]{:S(2)}, u32[]{:S(2)}) collective-permute-start(f32[32,1024]{1,0:T(8,128)S(1)} %dynamic-slice_add_fusion.1), channel_id=1, source_target_pairs={{0,192},{192,0},{64,128},{128,64},{1,193},{193,1},{65,129},{129,65... | collective-permute-start | bytes 393224 | tf_op jit(solution)/shard_map/ppermute | solution.py:386
  103.4 11.8 %collective-permute-start.19 = (f32[64,1024]{1,0:T(8,128)S(1)}, f32[64,1024]{1,0:T(8,128)S(1)}, u32[]{:S(2)}, u32[]{:S(2)}) collective-permute-start(f32[64,1024]{1,0:T(8,128)S(1)} %maximum_select_fusion.3), channel_id=1, source_target_pairs={{0,192},{192,0},{64,128},{128,64},{1,193},{193,1},{65,129},{129,65... | collective-permute-start | bytes 786440 | tf_op jit(solution)/shard_map/ppermute | solution.py:386
  106.8 8.5 %collective-permute-start.15 = (f32[64,1024]{1,0:T(8,128)S(1)}, f32[64,1024]{1,0:T(8,128)S(1)}, u32[]{:S(2)}, u32[]{:S(2)}) collective-permute-start(f32[64,1024]{1,0:T(8,128)S(1)} %maximum_select_fusion.2), channel_id=1, source_target_pairs={{0,64},{64,0},{128,192},{192,128},{1,65},{65,1},{129,193},{193,129... | collective-permute-start | bytes 786440 | tf_op jit(solution)/shard_map/ppermute | solution.py:386

commit v2 on v1

--- a/solution.py
+++ b/solution.py
@@ -8,6 +8,7 @@
 
 BLOCK = 128
 PIVOTS = 256
+STRIP = PIVOTS + BLOCK
 PLANE = ("frow", "fcol")
 ROWS = 16
 COLS = 4
@@ -125,8 +126,10 @@
         pivots[:BLOCK] = jnp.where(col <= row, k1_inv, k2_inv.T)
         pivots[BLOCK:PIVOTS] = -mm(k2_inv, mm(k21, k1_inv))
         pivots[PIVOTS : PIVOTS + BLOCK] = parent_inv
+        strip = mm_t(parent[pl.ds(pl.multiple_of(64 * leaf, 64), 64)], parent_inv)
+        pivots[STRIP : STRIP + 64] = jnp.where(leaf < 2, 0.0, strip)
         diag = jnp.sum(jnp.where(row == col, k2_inv, 0.0), axis=0, keepdims=True)
-        pivots[PIVOTS + BLOCK :] = jnp.broadcast_to(diag, (8, BLOCK))
+        pivots[STRIP + 64 :] = jnp.broadcast_to(diag, (8, BLOCK))
         k[:BLOCK, :BLOCK] = jnp.where(col <= row, mm_t(a11, k1_inv), 0.0)
         k[:BLOCK, BLOCK:] = jnp.zeros((BLOCK, BLOCK), jnp.float32)
         k[BLOCK:, :BLOCK] = k21
@@ -148,7 +151,7 @@
             pl.BlockSpec((PIVOTS, BLOCK), lambda i: (0, 0)),
         ],
         out_specs=[VMEM] * 8,
-        out_shape=[f32(392, BLOCK), f32(PIVOTS, PIVOTS), f32(BLOCK, BLOCK), f32(256, 384)]
+        out_shape=[f32(456, BLOCK), f32(PIVOTS, PIVOTS), f32(BLOCK, BLOCK), f32(256, 384)]
         + [f32(72, PIVOTS)] * 4,
         name="pack",
     )(front, parent)
@@ -166,7 +169,7 @@
     def _():
         row, col = square()
         both = pivots[:BLOCK]
-        diag = jnp.broadcast_to(pivots[PIVOTS + BLOCK : PIVOTS + BLOCK + 1], (BLOCK, BLOCK))
+        diag = jnp.broadcast_to(pivots[STRIP + 64 : STRIP + 65], (BLOCK, BLOCK))
         k_inv[:BLOCK, :BLOCK] = jnp.where(col <= row, both, 0.0)
         k_inv[:BLOCK, BLOCK:] = jnp.zeros((BLOCK, BLOCK), jnp.float32)
         k_inv[BLOCK:, :BLOCK] = pivots[BLOCK:PIVOTS]
@@ -222,7 +225,7 @@
     return pl.pallas_call(
         prepare_body,
         grid=(4,),
-        in_specs=[SMEM, whole(392, BLOCK), whole(BLOCK, BLOCK), whole(256, 384), FRONT, PARENT],
+        in_specs=[SMEM, whole(456, BLOCK), whole(BLOCK, BLOCK), whole(256, 384), FRONT, PARENT],
         out_specs=[
             PARENT,
             whole(256, 384),
@@ -240,7 +243,7 @@
     return jnp.concatenate([gathered[j, :64] for j in range(4)], axis=0)
 
 
-def contribute_body(maps, gathered, k_inv, kp_inv, base, high, low, *rest):
+def contribute_body(maps, gathered, first, k_inv, kp_inv, base, high, low, *rest):
     outs, (columns, value) = rest[:4], rest[4:]
     leaf, c = lax.axis_index("leaf"), lax.axis_index("fcol")
     i = pl.program_id(0)
@@ -258,9 +261,10 @@
     strip = jnp.concatenate(
         [gathered[j, 64:, half : half + BLOCK] for j in range(4) for half in (0, BLOCK)], axis=0
     )
-    pivot_strip = (c == 0) & (i == 0) & (leaf < 2)
     to = pl.multiple_of(64 * leaf, 64)
-    columns[pl.ds(to, 64), PIVOTS:] = mm_t(strip, kp_inv[...]) * jnp.where(pivot_strip, 0.0, 1.0)
+    columns[pl.ds(to, 64), PIVOTS:] = jnp.where(
+        (c == 0) & (i == 0), first[...], mm_t(strip, kp_inv[...])
+    )
     value[...] = base[...] - product_t((high[...], low[...]), halves(columns[...]))
     for half, bit in enumerate(first_bits(leaf)):
         for out, at_row in ((outs[2 * half], 1 - bit), (outs[2 * half + 1], bit)):
@@ -271,13 +275,14 @@
     return jnp.where((leaf == 1) | (leaf == 2), 1, 0), leaf // 2
 
 
-def contribute(maps, gathered, k_inv, kp_inv, base, high, low):
+def contribute(maps, gathered, pivots, k_inv, kp_inv, base, high, low):
     return pl.pallas_call(
         contribute_body,
         grid=(4,),
         in_specs=[
             SMEM,
             GATHERED,
+            pl.BlockSpec((64, BLOCK), lambda i: (STRIP // 64, 0)),
             whole(PIVOTS, PIVOTS),
             whole(BLOCK, BLOCK),
             PARENT,
@@ -288,7 +293,7 @@
         out_shape=[f32(64, 1024)] * 4,
         scratch_shapes=[pltpu.VMEM((256, 384), jnp.float32), pltpu.VMEM((256, 256), jnp.float32)],
         name="contribute",
-    )(maps, gathered, k_inv, kp_inv, base, high, low)
+    )(maps, gathered, pivots, k_inv, kp_inv, base, high, low)
 
 
 def finish_body(b_rows, gathered, k, k_inv, front, out, high, low):
@@ -360,7 +365,7 @@
 def scatter_columns(scattered):
     piece = None
     for j, sent in enumerate(scattered):
-        pairs = [(at(4 * k + i, 0), at(4 * i + j, k)) for k in range(COLS) for i in range(4)]
+        pairs = [(at(4 * k + i, 0), at(4 * i + j, k)) for k in range(COLS) for i in range(4) if k + i]
         got = lax.ppermute(sent, PLANE, pairs)
         piece = got if piece is None else piece + got
     return piece
@@ -374,11 +379,8 @@
 def sum_over_leaf(parts, leaf):
     near = [(0, 1), (1, 0), (2, 3), (3, 2)]
     far = [(0, 3), (3, 0), (1, 2), (2, 1)]
-    upper, lower = first_bits(leaf)
     sends, keeps = parts[0::2], parts[1::2]
     pairs = ((near, far), (far, near))
-    first = (upper, lower)
-    second = (leaf // 2, leaf % 2)
 
     def exchange(xs, turn):
         got = []
@@ -391,14 +393,10 @@
 
     got = exchange(sends, 0)
     sums = [x + y for x, y in zip(keeps, got)]
-    small = 32
-    cut = lambda x, i: lax.dynamic_slice_in_dim(x, i * small, small)
-    got = exchange([cut(x, 1 - b) for x, b in zip(sums, second)], 1)
-    done = [cut(x, b) + y for x, b, y in zip(sums, second, got)]
-    got = exchange(done, 1)
-    halved = [ordered(b, x, y) for b, x, y in zip(second, done, got)]
+    got = exchange(sums, 1)
+    halved = [x + y for x, y in zip(sums, got)]
     got = exchange(halved, 0)
-    return jnp.concatenate([ordered(b, x, y) for b, x, y in zip(first, halved, got)])
+    return jnp.concatenate([ordered(b, x, y) for b, x, y in zip(first_bits(leaf), halved, got)])
 
 
 def per_device(child_fronts, parent_front, block_maps):
@@ -417,7 +415,7 @@
     base, high, low, b_rows, k_inv, kp_inv = prepare(
         block_maps, pivots, kp, rows, child_fronts, parent_front
     )
-    parts = contribute(block_maps, gathered, k_inv, kp_inv, base, high, low)
+    parts = contribute(block_maps, gathered, pivots, k_inv, kp_inv, base, high, low)
     parent_done = sum_over_leaf(parts, leaf)
     finished = finish(b_rows, gathered, k, k_inv, child_fronts)
     return finished, parent_done

time: 117 us -> 116 us (level)
  the two profiles are of different devices: /device:TPU:46 before, /device:TPU:38 now
where the time goes in v2:
time: 116 us; the launch traced here: 115 us
  waiting for transfers between devices  57.7 us (50%)
  starting transfers between devices  29.1 us (25%)
  Pallas kernels  19.3 us (17%)
  other arithmetic  5.85 us (5%)
  local copies, waits for them, and re-layouts  2.13 us (2%)
    ppermute x2, waiting for transfers between devices, spread_far(): got = lax.ppermute(x, PLANE, [(at(q, 0), at(q, 2)) for q in range(ROWS)])  34.5 us
    ppermute x6, waiting for transfers between devices, exchange(): got.append(lax.ppermute(x, 'leaf', p[turn]))  14.7 us
    all_to_all x1, starting transfers between devices, gather_columns(): return lax.all_to_all(copies, 'frow', 0, 0, tiled=True)  10 us
    ppermute x4, waiting for transfers between devices, scatter_columns(): got = lax.ppermute(sent, PLANE, pairs)  8.35 us
    ppermute x6, starting transfers between devices, exchange(): got.append(lax.ppermute(x, 'leaf', p[turn]))  7.56 us
    pallas_call x1, Pallas kernels, contribute(): pl.pallas_call(contribute_body, grid=(4,), in_specs=[SMEM, GATHERED, pl.B...  6.56 us
    pallas_call x1, Pallas kernels, finish(): pl.pallas_call(finish_body, grid=(4,), in_specs=[whole(256, 384), GATHERE...  5.9 us
    pallas_call x1, Pallas kernels, prepare(): pl.pallas_call(prepare_body, grid=(4,), in_specs=[SMEM, whole(456, BLOCK)...  4.81 us
  transfers between devices with their start and end apart: 19, of which 8 were waited for; matrix products, arithmetic and copies ran while one was open for 5% of the time, Pallas kernels for 9%

profile of v2, /device:TPU:38, one launch (start us, length us, event | category | flops | bytes accessed | tf_op | source)
XLA Modules:
  0.0 115.0 jit_solution(4308884145863776757)
XLA Ops:
  0.6 2.1 %pack.1 = (f32[456,128]{1,0:T(8,128)}, f32[256,256]{1,0:T(8,128)}, f32[128,128]{1,0:T(8,128)}, f32[256,384]{1,0:T(8,128)}, f32[72,256]{1,0:T(8,128)}, /*index=5*...) custom-call(f32[1,256,1024]{2,1,0:T(8,128)} %front.5, f32[256,1024]{1,0:T(8,128)} %parent.3), custom_call_target="tpu_custom_call" | custom-call | tf_op jit(solution)/shard_map/pack/pallas_call | solution.py:146
  4.1 1.3 %collective-permute-start.11 = (f32[72,256]{1,0:T(8,128)}, f32[72,256]{1,0:T(8,128)S(1)}, u32[]{:S(2)}, u32[]{:S(2)}) collective-permute-start(f32[72,256]{1,0:T(8,128)} %get-tuple-element.27), channel_id=1, source_target_pairs={{4,28},{8,44},{12,60},{16,13},{20,29},{24,45},{28,61},{32,14},{36,... | collective-permute-start | bytes 221192 | tf_op jit(solution)/shard_map/ppermute | solution.py:369
  8.4 8.3 %collective-permute-done.11 = f32[72,256]{1,0:T(8,128)S(1)} collective-permute-done((f32[72,256]{1,0:T(8,128)}, f32[72,256]{1,0:T(8,128)S(1)}, u32[]{:S(2)}, u32[]{:S(2)}) %collective-permute-start.11) | collective-permute-done | bytes 73760 | tf_op jit(solution)/shard_map/ppermute | solution.py:369
  16.8 1.1 broadcast_in_dim.2
  17.9 10.0 %all-to-all-start = ((f32[16,72,256]{2,1,0:T(8,128)}), f32[16,72,256]{2,1,0:T(8,128)S(1)}, u32[]{:S(2)}, u32[]{:S(2)}) async-start(f32[16,72,256]{2,1,0:T(8,128)} %broadcast_in_dim.2), calls=%async_computation | async-start | bytes 2359296 | tf_op jit(solution)/shard_map/all_to_all | solution.py:376
  29.5 1.3 %collective-permute-start.6 = (f32[256,384]{1,0:T(8,128)S(1)}, f32[256,384]{1,0:T(8,128)S(1)}, u32[]{:S(2)}, u32[]{:S(2)}) collective-permute-start(f32[256,384]{1,0:T(8,128)S(1)} %copy-done.1), channel_id=1, source_target_pairs={{0,2},{4,6},{8,10},{12,14},{16,18},{20,22},{24,26},{28,30},{32,34}... | collective-permute-start | bytes 1179656 | tf_op jit(solution)/shard_map/ppermute | solution.py:356
  30.9 1.3 %collective-permute-start.4 = (f32[456,128]{1,0:T(8,128)S(1)}, f32[456,128]{1,0:T(8,128)S(1)}, u32[]{:S(2)}, u32[]{:S(2)}) collective-permute-start(f32[456,128]{1,0:T(8,128)S(1)} %broadcast_select_fusion.5), channel_id=1, source_target_pairs={{0,2},{4,6},{8,10},{12,14},{16,18},{20,22},{24,26},{28,30},{32,34}... | collective-permute-start | bytes 700424 | tf_op jit(solution)/shard_map/ppermute | solution.py:356
  32.2 13.5 %collective-permute-done.6 = f32[256,384]{1,0:T(8,128)S(1)} collective-permute-done((f32[256,384]{1,0:T(8,128)S(1)}, f32[256,384]{1,0:T(8,128)S(1)}, u32[]{:S(2)}, u32[]{:S(2)}) %collective-permute-start.6) | collective-permute-done | bytes 393248 | tf_op jit(solution)/shard_map/ppermute | solution.py:356
  45.7 1.3 %collective-permute-start.7 = (f32[256,384]{1,0:T(8,128)S(1)}, f32[256,384]{1,0:T(8,128)S(1)}, u32[]{:S(2)}, u32[]{:S(2)}) collective-permute-start(f32[256,384]{1,0:T(8,128)S(1)} %broadcast_select_fusion), channel_id=1, source_target_pairs={{0,1},{2,3},{4,5},{6,7},{8,9},{10,11},{12,13},{14,15},{16,17},{18,... | collective-permute-start | bytes 1179656 | tf_op jit(solution)/shard_map/ppermute | solution.py:361
  47.0 21.1 %collective-permute-done.4 = f32[456,128]{1,0:T(8,128)S(1)} collective-permute-done((f32[456,128]{1,0:T(8,128)S(1)}, f32[456,128]{1,0:T(8,128)S(1)}, u32[]{:S(2)}, u32[]{:S(2)}) %collective-permute-start.4) | collective-permute-done | bytes 233504 | tf_op jit(solution)/shard_map/ppermute | solution.py:356
  68.1 1.5 %collective-permute-start.5 = (f32[456,128]{1,0:T(8,128)S(1)}, f32[456,128]{1,0:T(8,128)S(1)}, u32[]{:S(2)}, u32[]{:S(2)}) collective-permute-start(f32[456,128]{1,0:T(8,128)S(1)} %broadcast_select_fusion.6), channel_id=1, source_target_pairs={{0,1},{2,3},{4,5},{6,7},{8,9},{10,11},{12,13},{14,15},{16,17},{18,... | collective-permute-start | bytes 700424 | tf_op jit(solution)/shard_map/ppermute | solution.py:361
  71.3 4.8 %prepare.1 = (f32[256,1024]{1,0:T(8,128)}, bf16[256,384]{1,0:T(8,128)(2,1)}, bf16[256,384]{1,0:T(8,128)(2,1)}, f32[256,384]{1,0:T(8,128)}, f32[256,256]{1,0:T(8,128)}, /*index=5*/f32[128,128]{1,0:T(8,128)}) custom-call(s32[1,32]{1,0:T(1,128)} %maps.3, f32[456,128]{1,0:T(8,128)} %broadcast_select_fusion.7.pivots.first, f32[128,128]{1,0:T(8,128)} %get-tuple-element.21.kp, ...), custom_call_target="tpu_custom_call" | custom-call | tf_op jit(solution)/shard_map/prepare/pallas_call | solution.py:225
  76.1 1.0 copy-done
  77.1 6.6 %contribute.1 = (f32[64,1024]{1,0:T(8,128)}, f32[64,1024]{1,0:T(8,128)}, f32[64,1024]{1,0:T(8,128)}, f32[64,1024]{1,0:T(8,128)}) custom-call(s32[1,32]{1,0:T(1,128)} %maps.3, f32[16,72,256]{2,1,0:T(8,128)} %copy-done, f32[456,128]{1,0:T(8,128)} %broadcast_select_fusion.7.pivots.first, f32[256,256]{1,0:T(8,128)} %get-tuple-element.29.k_inv, ...), custom_call_target="tpu_custom_call" | custom-call | tf_op jit(solution)/shard_map/contribute/pallas_call | solution.py:279
  83.7 1.6 %collective-permute-start.12 = (f32[64,1024]{1,0:T(8,128)}, f32[64,1024]{1,0:T(8,128)S(1)}, u32[]{:S(2)}, u32[]{:S(2)}) collective-permute-start(f32[64,1024]{1,0:T(8,128)} %get-tuple-element.35), channel_id=1, source_target_pairs={{0,64},{64,0},{128,192},{192,128},{1,65},{65,1},{129,193},{193,129... | collective-permute-start | bytes 786440 | tf_op jit(solution)/shard_map/ppermute | solution.py:388
  85.3 2.2 %collective-permute-start.15 = (f32[64,1024]{1,0:T(8,128)}, f32[64,1024]{1,0:T(8,128)S(1)}, u32[]{:S(2)}, u32[]{:S(2)}) collective-permute-start(f32[64,1024]{1,0:T(8,128)} %get-tuple-element.37), channel_id=1, source_target_pairs={{0,192},{192,0},{64,128},{128,64},{1,193},{193,1},{65,129},{129,65... | collective-permute-start | bytes 786440 | tf_op jit(solution)/shard_map/ppermute | solution.py:388
  87.5 5.1 %collective-permute-done.12 = f32[64,1024]{1,0:T(8,128)S(1)} collective-permute-done((f32[64,1024]{1,0:T(8,128)}, f32[64,1024]{1,0:T(8,128)S(1)}, u32[]{:S(2)}, u32[]{:S(2)}) %collective-permute-start.12) | collective-permute-done | bytes 262176 | tf_op jit(solution)/shard_map/ppermute | solution.py:388
  93.5 3.1 %collective-permute-start.13 = (f32[64,1024]{1,0:T(8,128)S(1)}, f32[64,1024]{1,0:T(8,128)S(1)}, u32[]{:S(2)}, u32[]{:S(2)}) collective-permute-start(f32[64,1024]{1,0:T(8,128)S(1)} %add.47), channel_id=1, source_target_pairs={{0,192},{192,0},{64,128},{128,64},{1,193},{193,1},{65,129},{129,65... | collective-permute-start | bytes 786440 | tf_op jit(solution)/shard_map/ppermute | solution.py:388
  96.6 1.0 add.49
  97.8 4.8 %collective-permute-done.13 = f32[64,1024]{1,0:T(8,128)S(1)} collective-permute-done((f32[64,1024]{1,0:T(8,128)S(1)}, f32[64,1024]{1,0:T(8,128)S(1)}, u32[]{:S(2)}, u32[]{:S(2)}) %collective-permute-start.13) | collective-permute-done | bytes 262176 | tf_op jit(solution)/shard_map/ppermute | solution.py:388
  103.0 3.2 %collective-permute-done.16 = f32[64,1024]{1,0:T(8,128)S(1)} collective-permute-done((f32[64,1024]{1,0:T(8,128)S(1)}, f32[64,1024]{1,0:T(8,128)S(1)}, u32[]{:S(2)}, u32[]{:S(2)}) %collective-permute-start.16) | collective-permute-done | bytes 262176 | tf_op jit(solution)/shard_map/ppermute | solution.py:388
  106.4 5.9 %finish.1 = f32[1,256,1024]{2,1,0:T(8,128)} custom-call(f32[256,384]{1,0:T(8,128)} %get-tuple-element.23.b_rows, f32[16,72,256]{2,1,0:T(8,128)} %copy-done, f32[256,256]{1,0:T(8,128)} %get-tuple-element.28.k, f32[256,256]{1,0:T(8,128)} %get-tuple-element.29.k_inv, f32[1,256,1024]{2,1,0:T(8,128)} %front.5), custom_call_target="tpu_custom_call" | custom-call | flops 2147483648 | bytes 4194304 | tf_op jit(solution)/shard_map/finish/pallas_call | solution.py:322
  112.3 1.6 %collective-permute-done.17 = f32[64,1024]{1,0:T(8,128)S(1)} collective-permute-done((f32[64,1024]{1,0:T(8,128)S(1)}, f32[64,1024]{1,0:T(8,128)S(1)}, u32[]{:S(2)}, u32[]{:S(2)}) %collective-permute-start.17) | collective-permute-done | bytes 262176 | tf_op jit(solution)/shard_map/ppermute | solution.py:388
  114.0 1.0 pad_maximum_fusion
  (39 shorter events, 9.5 us)
Async XLA Ops:
  2.7 4.0 %collective-permute-start = (f32[456,128]{1,0:T(8,128)}, f32[456,128]{1,0:T(8,128)S(1)}, u32[]{:S(2)}, u32[]{:S(2)}) collective-permute-start(f32[456,128]{1,0:T(8,128)} %get-tuple-element.20), channel_id=1, source_target_pairs={{0,32},{64,96},{128,160},{192,224}} | collective-permute-start | bytes 700424 | tf_op jit(solution)/shard_map/ppermute | solution.py:350
  3.4 5.0 %collective-permute-start.10 = (f32[72,256]{1,0:T(8,128)}, f32[72,256]{1,0:T(8,128)S(1)}, u32[]{:S(2)}, u32[]{:S(2)}) collective-permute-start(f32[72,256]{1,0:T(8,128)} %get-tuple-element.26), channel_id=1, source_target_pairs={{4,24},{8,40},{12,56},{16,9},{20,25},{24,41},{28,57},{32,10},{36,2... | collective-permute-start | bytes 221192 | tf_op jit(solution)/shard_map/ppermute | solution.py:369
  4.1 12.7 %collective-permute-start.11 = (f32[72,256]{1,0:T(8,128)}, f32[72,256]{1,0:T(8,128)S(1)}, u32[]{:S(2)}, u32[]{:S(2)}) collective-permute-start(f32[72,256]{1,0:T(8,128)} %get-tuple-element.27), channel_id=1, source_target_pairs={{4,28},{8,44},{12,60},{16,13},{20,29},{24,45},{28,61},{32,14},{36,... | collective-permute-start | bytes 221192 | tf_op jit(solution)/shard_map/ppermute | solution.py:369
  5.4 11.4 %collective-permute-start.8 = (f32[72,256]{1,0:T(8,128)}, f32[72,256]{1,0:T(8,128)S(1)}, u32[]{:S(2)}, u32[]{:S(2)}) collective-permute-start(f32[72,256]{1,0:T(8,128)} %get-tuple-element.24), channel_id=1, source_target_pairs={{4,16},{8,32},{12,48},{16,1},{20,17},{24,33},{28,49},{32,2},{36,18... | collective-permute-start | bytes 221192 | tf_op jit(solution)/shard_map/ppermute | solution.py:369
  6.0 10.7 %collective-permute-start.9 = (f32[72,256]{1,0:T(8,128)}, f32[72,256]{1,0:T(8,128)S(1)}, u32[]{:S(2)}, u32[]{:S(2)}) collective-permute-start(f32[72,256]{1,0:T(8,128)} %get-tuple-element.25), channel_id=1, source_target_pairs={{4,20},{8,36},{12,52},{16,5},{20,21},{24,37},{28,53},{32,6},{36,22... | collective-permute-start | bytes 221192 | tf_op jit(solution)/shard_map/ppermute | solution.py:369
  7.7 20.2 %collective-permute-start.1 = (f32[456,128]{1,0:T(8,128)S(1)}, f32[456,128]{1,0:T(8,128)S(1)}, u32[]{:S(2)}, u32[]{:S(2)}) collective-permute-start(f32[456,128]{1,0:T(8,128)S(1)} %broadcast_select_fusion.2), channel_id=1, source_target_pairs={{0,16},{32,48},{64,80},{96,112},{128,144},{160,176},{192,208},{224... | collective-permute-start | bytes 700424 | tf_op jit(solution)/shard_map/ppermute | solution.py:350
  17.9 58.2 %all-to-all-start = ((f32[16,72,256]{2,1,0:T(8,128)}), f32[16,72,256]{2,1,0:T(8,128)S(1)}, u32[]{:S(2)}, u32[]{:S(2)}) async-start(f32[16,72,256]{2,1,0:T(8,128)} %broadcast_in_dim.2), calls=%async_computation | async-start | bytes 2359296 | tf_op jit(solution)/shard_map/all_to_all | solution.py:376
  27.9 1.6 %copy-start.1 = (f32[256,384]{1,0:T(8,128)S(1)}, f32[256,384]{1,0:T(8,128)}, u32[]{:S(2)}) copy-start(f32[256,384]{1,0:T(8,128)} %get-tuple-element.22) | copy-start | bytes 1179652
  27.9 0.8 collective-permute-start.2
  28.8 2.0 %collective-permute-start.3 = (f32[456,128]{1,0:T(8,128)S(1)}, f32[456,128]{1,0:T(8,128)S(1)}, u32[]{:S(2)}, u32[]{:S(2)}) collective-permute-start(f32[456,128]{1,0:T(8,128)S(1)} %broadcast_select_fusion.4), channel_id=1, source_target_pairs={{0,4},{8,12},{16,20},{24,28},{32,36},{40,44},{48,52},{56,60},{64,6... | collective-permute-start | bytes 700424 | tf_op jit(solution)/shard_map/ppermute | solution.py:350
  29.5 16.1 %collective-permute-start.6 = (f32[256,384]{1,0:T(8,128)S(1)}, f32[256,384]{1,0:T(8,128)S(1)}, u32[]{:S(2)}, u32[]{:S(2)}) collective-permute-start(f32[256,384]{1,0:T(8,128)S(1)} %copy-done.1), channel_id=1, source_target_pairs={{0,2},{4,6},{8,10},{12,14},{16,18},{20,22},{24,26},{28,30},{32,34}... | collective-permute-start | bytes 1179656 | tf_op jit(solution)/shard_map/ppermute | solution.py:356
  30.9 37.2 %collective-permute-start.4 = (f32[456,128]{1,0:T(8,128)S(1)}, f32[456,128]{1,0:T(8,128)S(1)}, u32[]{:S(2)}, u32[]{:S(2)}) collective-permute-start(f32[456,128]{1,0:T(8,128)S(1)} %broadcast_select_fusion.5), channel_id=1, source_target_pairs={{0,2},{4,6},{8,10},{12,14},{16,18},{20,22},{24,26},{28,30},{32,34}... | collective-permute-start | bytes 700424 | tf_op jit(solution)/shard_map/ppermute | solution.py:356
  45.7 23.9 %collective-permute-start.7 = (f32[256,384]{1,0:T(8,128)S(1)}, f32[256,384]{1,0:T(8,128)S(1)}, u32[]{:S(2)}, u32[]{:S(2)}) collective-permute-start(f32[256,384]{1,0:T(8,128)S(1)} %broadcast_select_fusion), channel_id=1, source_target_pairs={{0,1},{2,3},{4,5},{6,7},{8,9},{10,11},{12,13},{14,15},{16,17},{18,... | collective-permute-start | bytes 1179656 | tf_op jit(solution)/shard_map/ppermute | solution.py:361
  68.1 2.4 %collective-permute-start.5 = (f32[456,128]{1,0:T(8,128)S(1)}, f32[456,128]{1,0:T(8,128)S(1)}, u32[]{:S(2)}, u32[]{:S(2)}) collective-permute-start(f32[456,128]{1,0:T(8,128)S(1)} %broadcast_select_fusion.6), channel_id=1, source_target_pairs={{0,1},{2,3},{4,5},{6,7},{8,9},{10,11},{12,13},{14,15},{16,17},{18,... | collective-permute-start | bytes 700424 | tf_op jit(solution)/shard_map/ppermute | solution.py:361
  76.1 1.0 copy-start
  83.7 8.9 %collective-permute-start.12 = (f32[64,1024]{1,0:T(8,128)}, f32[64,1024]{1,0:T(8,128)S(1)}, u32[]{:S(2)}, u32[]{:S(2)}) collective-permute-start(f32[64,1024]{1,0:T(8,128)} %get-tuple-element.35), channel_id=1, source_target_pairs={{0,64},{64,0},{128,192},{192,128},{1,65},{65,1},{129,193},{193,129... | collective-permute-start | bytes 786440 | tf_op jit(solution)/shard_map/ppermute | solution.py:388
  85.3 11.3 %collective-permute-start.15 = (f32[64,1024]{1,0:T(8,128)}, f32[64,1024]{1,0:T(8,128)S(1)}, u32[]{:S(2)}, u32[]{:S(2)}) collective-permute-start(f32[64,1024]{1,0:T(8,128)} %get-tuple-element.37), channel_id=1, source_target_pairs={{0,192},{192,0},{64,128},{128,64},{1,193},{193,1},{65,129},{129,65... | collective-permute-start | bytes 786440 | tf_op jit(solution)/shard_map/ppermute | solution.py:388
  93.5 9.1 %collective-permute-start.13 = (f32[64,1024]{1,0:T(8,128)S(1)}, f32[64,1024]{1,0:T(8,128)S(1)}, u32[]{:S(2)}, u32[]{:S(2)}) collective-permute-start(f32[64,1024]{1,0:T(8,128)S(1)} %add.47), channel_id=1, source_target_pairs={{0,192},{192,0},{64,128},{128,64},{1,193},{193,1},{65,129},{129,65... | collective-permute-start | bytes 786440 | tf_op jit(solution)/shard_map/ppermute | solution.py:388
  97.6 8.7 %collective-permute-start.16 = (f32[64,1024]{1,0:T(8,128)S(1)}, f32[64,1024]{1,0:T(8,128)S(1)}, u32[]{:S(2)}, u32[]{:S(2)}) collective-permute-start(f32[64,1024]{1,0:T(8,128)S(1)} %add.49), channel_id=1, source_target_pairs={{0,64},{64,0},{128,192},{192,128},{1,65},{65,1},{129,193},{193,129... | collective-permute-start | bytes 786440 | tf_op jit(solution)/shard_map/ppermute | solution.py:388
  102.6 9.7 %collective-permute-start.14 = (f32[64,1024]{1,0:T(8,128)S(1)}, f32[64,1024]{1,0:T(8,128)S(1)}, u32[]{:S(2)}, u32[]{:S(2)}) collective-permute-start(f32[64,1024]{1,0:T(8,128)S(1)} %add.48), channel_id=1, source_target_pairs={{0,64},{64,0},{128,192},{192,128},{1,65},{65,1},{129,193},{193,129... | collective-permute-start | bytes 786440 | tf_op jit(solution)/shard_map/ppermute | solution.py:388
  106.3 7.7 %collective-permute-start.17 = (f32[64,1024]{1,0:T(8,128)S(1)}, f32[64,1024]{1,0:T(8,128)S(1)}, u32[]{:S(2)}, u32[]{:S(2)}) collective-permute-start(f32[64,1024]{1,0:T(8,128)S(1)} %add.50), channel_id=1, source_target_pairs={{0,192},{192,0},{64,128},{128,64},{1,193},{193,1},{65,129},{129,65... | collective-permute-start | bytes 786440 | tf_op jit(solution)/shard_map/ppermute | solution.py:388

commit v3 on v2

--- a/solution.py
+++ b/solution.py
@@ -293,6 +293,7 @@
         out_shape=[f32(64, 1024)] * 4,
         scratch_shapes=[pltpu.VMEM((256, 384), jnp.float32), pltpu.VMEM((256, 256), jnp.float32)],
         name="contribute",
+        compiler_params=pltpu.CompilerParams(vmem_limit_bytes=24 << 20),
     )(maps, gathered, pivots, k_inv, kp_inv, base, high, low)
 
 
@@ -337,6 +338,7 @@
         ],
         cost_estimate=pl.CostEstimate(flops=1 << 31, bytes_accessed=4 << 20, transcendentals=0),
         name="finish",
+        compiler_params=pltpu.CompilerParams(vmem_limit_bytes=24 << 20),
     )(b_rows, gathered, k, k_inv, front)
 
 
@@ -415,7 +417,8 @@
     base, high, low, b_rows, k_inv, kp_inv = prepare(
         block_maps, pivots, kp, rows, child_fronts, parent_front
     )
-    parts = contribute(block_maps, gathered, pivots, k_inv, kp_inv, base, high, low)
+    in_hbm = [pltpu.with_memory_space_constraint(x, pltpu.HBM) for x in (pivots, k_inv, kp_inv, base, high, low)]
+    parts = contribute(block_maps, gathered, *in_hbm)
     parent_done = sum_over_leaf(parts, leaf)
     finished = finish(b_rows, gathered, k, k_inv, child_fronts)
     return finished, parent_done

time: 116 us -> 112 us (0.966)
  waiting for transfers between devices: 57.7 us -> 54.4 us
  Pallas kernels: 19.3 us -> 17.2 us
  starting transfers between devices: 29.1 us -> 30.9 us
    ppermute x6, waiting for transfers between devices: 14.7 us -> 11.4 us  [exchange(): got.append(lax.ppermute(x, 'leaf', p[turn]))]
    add x2, other arithmetic: 1.98 us -> 0.06 us  [sum_over_leaf(): sums = [x + y for x, y in zip(keeps, got)]]
    ppermute x6, starting transfers between devices: 7.56 us -> 9.45 us  [exchange(): got.append(lax.ppermute(x, 'leaf', p[turn]))]
    add x2, other arithmetic: 0.07 us -> 1.71 us  [sum_over_leaf(): halved = [x + y for x, y in zip(sums, got)]]
    pallas_call x1, Pallas kernels: 5.9 us -> 4.4 us  [finish(): pl.pallas_call(finish_body, grid=(4,), in_specs=[whole(256, 384), GATHERE...]
    select_n x2, other arithmetic: 0.09 us -> 1.28 us  [ordered(): jnp.where(bit == 0, jnp.concatenate([mine, got]), jnp.concatenate([got, m...]
  transfers between devices with their start and end apart: 19 -> 19, of which waited for: 8 -> 8; matrix products, arithmetic and copies ran while one was open for 5% -> 6% of each run, Pallas kernels for 9% -> 8%
where the time goes in v3:
time: 112 us; the launch traced here: 111 us
  waiting for transfers between devices  54.4 us (49%)
  starting transfers between devices  30.9 us (28%)
  Pallas kernels  17.2 us (15%)
  other arithmetic  6.76 us (6%)
  local copies, waits for them, and re-layouts  1.15 us (1%)
    ppermute x2, waiting for transfers between devices, spread_far(): got = lax.ppermute(x, PLANE, [(at(q, 0), at(q, 2)) for q in range(ROWS)])  34.5 us
    ppermute x6, waiting for transfers between devices, exchange(): got.append(lax.ppermute(x, 'leaf', p[turn]))  11.4 us
    all_to_all x1, starting transfers between devices, gather_columns(): return lax.all_to_all(copies, 'frow', 0, 0, tiled=True)  10 us
    ppermute x6, starting transfers between devices, exchange(): got.append(lax.ppermute(x, 'leaf', p[turn]))  9.45 us
    ppermute x4, waiting for transfers between devices, scatter_columns(): got = lax.ppermute(sent, PLANE, pairs)  8.35 us
    pallas_call x1, Pallas kernels, contribute(): pl.pallas_call(contribute_body, grid=(4,), in_specs=[SMEM, GATHERED, pl.B...  5.91 us
    pallas_call x1, Pallas kernels, prepare(): pl.pallas_call(prepare_body, grid=(4,), in_specs=[SMEM, whole(456, BLOCK)...  4.83 us
    pallas_call x1, Pallas kernels, finish(): pl.pallas_call(finish_body, grid=(4,), in_specs=[whole(256, 384), GATHERE...  4.4 us
  transfers between devices with their start and end apart: 19, of which 8 were waited for; matrix products, arithmetic and copies ran while one was open for 6% of the time, Pallas kernels for 8%

profile of v3, /device:TPU:38, one launch (start us, length us, event | category | flops | bytes accessed | tf_op | source)
XLA Modules:
  0.0 111.5 jit_solution(6246822611014959246)
XLA Ops:
  0.6 2.1 %pack.1 = (f32[456,128]{1,0:T(8,128)}, f32[256,256]{1,0:T(8,128)}, f32[128,128]{1,0:T(8,128)}, f32[256,384]{1,0:T(8,128)}, f32[72,256]{1,0:T(8,128)}, /*index=5*...) custom-call(f32[1,256,1024]{2,1,0:T(8,128)} %front.5, f32[256,1024]{1,0:T(8,128)} %parent.3), custom_call_target="tpu_custom_call" | custom-call | tf_op jit(solution)/shard_map/pack/pallas_call | solution.py:146
  4.1 1.3 %collective-permute-start.11 = (f32[72,256]{1,0:T(8,128)}, f32[72,256]{1,0:T(8,128)S(1)}, u32[]{:S(2)}, u32[]{:S(2)}) collective-permute-start(f32[72,256]{1,0:T(8,128)} %get-tuple-element.27), channel_id=1, source_target_pairs={{4,28},{8,44},{12,60},{16,13},{20,29},{24,45},{28,61},{32,14},{36,... | collective-permute-start | bytes 221192 | tf_op jit(solution)/shard_map/ppermute | solution.py:371
  6.7 1.0 broadcast_select_fusion.2
  8.4 8.3 %collective-permute-done.11 = f32[72,256]{1,0:T(8,128)S(1)} collective-permute-done((f32[72,256]{1,0:T(8,128)}, f32[72,256]{1,0:T(8,128)S(1)}, u32[]{:S(2)}, u32[]{:S(2)}) %collective-permute-start.11) | collective-permute-done | bytes 73760 | tf_op jit(solution)/shard_map/ppermute | solution.py:371
  16.8 1.1 %broadcast_in_dim.2 = f32[16,72,256]{2,1,0:T(8,128)} broadcast(f32[72,256]{1,0:T(8,128)S(1)} %add_add_fusion), dimensions={1,2} | broadcast | bytes 1253376 | tf_op jit(solution)/shard_map/broadcast_in_dim | solution.py:377
  17.9 10.0 %all-to-all-start = ((f32[16,72,256]{2,1,0:T(8,128)}), f32[16,72,256]{2,1,0:T(8,128)S(1)}, u32[]{:S(2)}, u32[]{:S(2)}) async-start(f32[16,72,256]{2,1,0:T(8,128)} %broadcast_in_dim.2), calls=%async_computation | async-start | bytes 2359296 | tf_op jit(solution)/shard_map/all_to_all | solution.py:378
  29.5 1.3 %collective-permute-start.6 = (f32[256,384]{1,0:T(8,128)S(1)}, f32[256,384]{1,0:T(8,128)S(1)}, u32[]{:S(2)}, u32[]{:S(2)}) collective-permute-start(f32[256,384]{1,0:T(8,128)S(1)} %copy-done.5), channel_id=1, source_target_pairs={{0,2},{4,6},{8,10},{12,14},{16,18},{20,22},{24,26},{28,30},{32,34}... | collective-permute-start | bytes 1179656 | tf_op jit(solution)/shard_map/ppermute | solution.py:358
  30.9 1.3 %collective-permute-start.4 = (f32[456,128]{1,0:T(8,128)S(1)}, f32[456,128]{1,0:T(8,128)S(1)}, u32[]{:S(2)}, u32[]{:S(2)}) collective-permute-start(f32[456,128]{1,0:T(8,128)S(1)} %broadcast_select_fusion.5), channel_id=1, source_target_pairs={{0,2},{4,6},{8,10},{12,14},{16,18},{20,22},{24,26},{28,30},{32,34}... | collective-permute-start | bytes 700424 | tf_op jit(solution)/shard_map/ppermute | solution.py:358
  32.2 13.5 %collective-permute-done.6 = f32[256,384]{1,0:T(8,128)S(1)} collective-permute-done((f32[256,384]{1,0:T(8,128)S(1)}, f32[256,384]{1,0:T(8,128)S(1)}, u32[]{:S(2)}, u32[]{:S(2)}) %collective-permute-start.6) | collective-permute-done | bytes 393248 | tf_op jit(solution)/shard_map/ppermute | solution.py:358
  45.7 1.3 %collective-permute-start.7 = (f32[256,384]{1,0:T(8,128)S(1)}, f32[256,384]{1,0:T(8,128)S(1)}, u32[]{:S(2)}, u32[]{:S(2)}) collective-permute-start(f32[256,384]{1,0:T(8,128)S(1)} %broadcast_select_fusion), channel_id=1, source_target_pairs={{0,1},{2,3},{4,5},{6,7},{8,9},{10,11},{12,13},{14,15},{16,17},{18,... | collective-permute-start | bytes 1179656 | tf_op jit(solution)/shard_map/ppermute | solution.py:363
  47.1 21.1 %collective-permute-done.4 = f32[456,128]{1,0:T(8,128)S(1)} collective-permute-done((f32[456,128]{1,0:T(8,128)S(1)}, f32[456,128]{1,0:T(8,128)S(1)}, u32[]{:S(2)}, u32[]{:S(2)}) %collective-permute-start.4) | collective-permute-done | bytes 233504 | tf_op jit(solution)/shard_map/ppermute | solution.py:358
  68.2 1.5 %collective-permute-start.5 = (f32[456,128]{1,0:T(8,128)S(1)}, f32[456,128]{1,0:T(8,128)S(1)}, u32[]{:S(2)}, u32[]{:S(2)}) collective-permute-start(f32[456,128]{1,0:T(8,128)S(1)} %broadcast_select_fusion.6), channel_id=1, source_target_pairs={{0,1},{2,3},{4,5},{6,7},{8,9},{10,11},{12,13},{14,15},{16,17},{18,... | collective-permute-start | bytes 700424 | tf_op jit(solution)/shard_map/ppermute | solution.py:363
  71.3 4.8 %prepare.1 = (f32[256,1024]{1,0:T(8,128)}, bf16[256,384]{1,0:T(8,128)(2,1)}, bf16[256,384]{1,0:T(8,128)(2,1)}, f32[256,384]{1,0:T(8,128)}, f32[256,256]{1,0:T(8,128)}, /*index=5*/f32[128,128]{1,0:T(8,128)}) custom-call(s32[1,32]{1,0:T(1,128)} %maps.3, f32[456,128]{1,0:T(8,128)} %broadcast_select_fusion.7.pivots.first, f32[128,128]{1,0:T(8,128)} %get-tuple-element.21.kp, ...), custom_call_target="tpu_custom_call" | custom-call | tf_op jit(solution)/shard_map/prepare/pallas_call | solution.py:225
  76.1 5.9 %contribute.1 = (f32[64,1024]{1,0:T(8,128)S(1)}, f32[64,1024]{1,0:T(8,128)S(1)}, f32[64,1024]{1,0:T(8,128)S(1)}, f32[64,1024]{1,0:T(8,128)S(1)}) custom-call(s32[1,32]{1,0:T(1,128)S(1)} %copy-done.2, f32[16,72,256]{2,1,0:T(8,128)S(1)} %all-to-all-done.gathered, f32[456,128]{1,0:T(8,128)} %broadcast_select_fusion.7.pivots.first, ...), custom_call_target="tpu_custom_call" | custom-call | tf_op jit(solution)/shard_map/contribute/pallas_call | solution.py:279
  82.1 1.6 %collective-permute-start.12 = (f32[64,1024]{1,0:T(8,128)S(1)}, f32[64,1024]{1,0:T(8,128)S(1)}, u32[]{:S(2)}, u32[]{:S(2)}) collective-permute-start(f32[64,1024]{1,0:T(8,128)S(1)} %get-tuple-element.35), channel_id=1, source_target_pairs={{0,64},{64,0},{128,192},{192,128},{1,65},{65,1},{129,193},{193,129... | collective-permute-start | bytes 786440 | tf_op jit(solution)/shard_map/ppermute | solution.py:390
  83.7 2.2 %collective-permute-start.15 = (f32[64,1024]{1,0:T(8,128)S(1)}, f32[64,1024]{1,0:T(8,128)S(1)}, u32[]{:S(2)}, u32[]{:S(2)}) collective-permute-start(f32[64,1024]{1,0:T(8,128)S(1)} %get-tuple-element.37), channel_id=1, source_target_pairs={{0,192},{192,0},{64,128},{128,64},{1,193},{193,1},{65,129},{129,65... | collective-permute-start | bytes 786440 | tf_op jit(solution)/shard_map/ppermute | solution.py:390
  85.9 4.9 %collective-permute-done.12 = f32[64,1024]{1,0:T(8,128)S(1)} collective-permute-done((f32[64,1024]{1,0:T(8,128)S(1)}, f32[64,1024]{1,0:T(8,128)S(1)}, u32[]{:S(2)}, u32[]{:S(2)}) %collective-permute-start.12) | collective-permute-done | bytes 262176 | tf_op jit(solution)/shard_map/ppermute | solution.py:390
  90.8 3.1 %collective-permute-start.13 = (f32[64,1024]{1,0:T(8,128)S(1)}, f32[64,1024]{1,0:T(8,128)S(1)}, u32[]{:S(2)}, u32[]{:S(2)}) collective-permute-start(f32[64,1024]{1,0:T(8,128)S(1)} %add.47), channel_id=1, source_target_pairs={{0,192},{192,0},{64,128},{128,64},{1,193},{193,1},{65,129},{129,65... | collective-permute-start | bytes 786440 | tf_op jit(solution)/shard_map/ppermute | solution.py:390
  94.1 5.7 %collective-permute-done.13 = f32[64,1024]{1,0:T(8,128)S(1)} collective-permute-done((f32[64,1024]{1,0:T(8,128)S(1)}, f32[64,1024]{1,0:T(8,128)S(1)}, u32[]{:S(2)}, u32[]{:S(2)}) %collective-permute-start.13) | collective-permute-done | bytes 262176 | tf_op jit(solution)/shard_map/ppermute | solution.py:390
  101.5 1.0 add.50
  102.5 2.1 %collective-permute-start.17 = (f32[64,1024]{1,0:T(8,128)S(1)}, f32[64,1024]{1,0:T(8,128)S(1)}, u32[]{:S(2)}, u32[]{:S(2)}) collective-permute-start(f32[64,1024]{1,0:T(8,128)S(1)} %add.50), channel_id=1, source_target_pairs={{0,192},{192,0},{64,128},{128,64},{1,193},{193,1},{65,129},{129,65... | collective-permute-start | bytes 786440 | tf_op jit(solution)/shard_map/ppermute | solution.py:390
  104.6 4.4 %finish.1 = f32[1,256,1024]{2,1,0:T(8,128)} custom-call(f32[256,384]{1,0:T(8,128)S(1)} %copy-done.3, f32[16,72,256]{2,1,0:T(8,128)S(1)} %all-to-all-done.gathered, f32[256,256]{1,0:T(8,128)S(1)} %copy-done.4, f32[256,256]{1,0:T(8,128)S(1)} %copy-done.1, f32[1,256,1024]{2,1,0:T(8,128)S(1)} %copy-done), custom_call_target="tpu_custom_call" | custom-call | flops 2147483648 | bytes 4194304 | tf_op jit(solution)/shard_map/finish/pallas_call | solution.py:323
  109.0 1.2 %maximum_select_fusion = f32[128,1024]{1,0:T(8,128)S(1)} fusion(f32[64,1024]{1,0:T(8,128)} %collective-permute-done.14, f32[64,1024]{1,0:T(8,128)} %add.48, pred[]{:T(512)S(6)} %eq.47), kind=kLoop, calls=%fused_computation.1 | loop fusion | flops 393216 | bytes 1048577 | tf_op jit(solution)/shard_map/jit(_where)/select_n | solution.py:394
  110.4 1.0 pad_maximum_fusion
  (47 shorter events, 8.8 us)
Async XLA Ops:
  2.7 4.0 %collective-permute-start = (f32[456,128]{1,0:T(8,128)}, f32[456,128]{1,0:T(8,128)S(1)}, u32[]{:S(2)}, u32[]{:S(2)}) collective-permute-start(f32[456,128]{1,0:T(8,128)} %get-tuple-element.20), channel_id=1, source_target_pairs={{0,32},{64,96},{128,160},{192,224}} | collective-permute-start | bytes 700424 | tf_op jit(solution)/shard_map/ppermute | solution.py:352
  3.4 5.0 %collective-permute-start.10 = (f32[72,256]{1,0:T(8,128)}, f32[72,256]{1,0:T(8,128)S(1)}, u32[]{:S(2)}, u32[]{:S(2)}) collective-permute-start(f32[72,256]{1,0:T(8,128)} %get-tuple-element.26), channel_id=1, source_target_pairs={{4,24},{8,40},{12,56},{16,9},{20,25},{24,41},{28,57},{32,10},{36,2... | collective-permute-start | bytes 221192 | tf_op jit(solution)/shard_map/ppermute | solution.py:371
  4.1 12.7 %collective-permute-start.11 = (f32[72,256]{1,0:T(8,128)}, f32[72,256]{1,0:T(8,128)S(1)}, u32[]{:S(2)}, u32[]{:S(2)}) collective-permute-start(f32[72,256]{1,0:T(8,128)} %get-tuple-element.27), channel_id=1, source_target_pairs={{4,28},{8,44},{12,60},{16,13},{20,29},{24,45},{28,61},{32,14},{36,... | collective-permute-start | bytes 221192 | tf_op jit(solution)/shard_map/ppermute | solution.py:371
  5.4 11.4 %collective-permute-start.8 = (f32[72,256]{1,0:T(8,128)}, f32[72,256]{1,0:T(8,128)S(1)}, u32[]{:S(2)}, u32[]{:S(2)}) collective-permute-start(f32[72,256]{1,0:T(8,128)} %get-tuple-element.24), channel_id=1, source_target_pairs={{4,16},{8,32},{12,48},{16,1},{20,17},{24,33},{28,49},{32,2},{36,18... | collective-permute-start | bytes 221192 | tf_op jit(solution)/shard_map/ppermute | solution.py:371
  6.0 10.7 %collective-permute-start.9 = (f32[72,256]{1,0:T(8,128)}, f32[72,256]{1,0:T(8,128)S(1)}, u32[]{:S(2)}, u32[]{:S(2)}) collective-permute-start(f32[72,256]{1,0:T(8,128)} %get-tuple-element.25), channel_id=1, source_target_pairs={{4,20},{8,36},{12,52},{16,5},{20,21},{24,37},{28,53},{32,6},{36,22... | collective-permute-start | bytes 221192 | tf_op jit(solution)/shard_map/ppermute | solution.py:371
  7.7 20.2 %collective-permute-start.1 = (f32[456,128]{1,0:T(8,128)S(1)}, f32[456,128]{1,0:T(8,128)S(1)}, u32[]{:S(2)}, u32[]{:S(2)}) collective-permute-start(f32[456,128]{1,0:T(8,128)S(1)} %broadcast_select_fusion.2), channel_id=1, source_target_pairs={{0,16},{32,48},{64,80},{96,112},{128,144},{160,176},{192,208},{224... | collective-permute-start | bytes 700424 | tf_op jit(solution)/shard_map/ppermute | solution.py:352
  17.9 58.2 %all-to-all-start = ((f32[16,72,256]{2,1,0:T(8,128)}), f32[16,72,256]{2,1,0:T(8,128)S(1)}, u32[]{:S(2)}, u32[]{:S(2)}) async-start(f32[16,72,256]{2,1,0:T(8,128)} %broadcast_in_dim.2), calls=%async_computation | async-start | bytes 2359296 | tf_op jit(solution)/shard_map/all_to_all | solution.py:378
  28.0 0.8 collective-permute-start.2
  28.8 2.0 %collective-permute-start.3 = (f32[456,128]{1,0:T(8,128)S(1)}, f32[456,128]{1,0:T(8,128)S(1)}, u32[]{:S(2)}, u32[]{:S(2)}) collective-permute-start(f32[456,128]{1,0:T(8,128)S(1)} %broadcast_select_fusion.4), channel_id=1, source_target_pairs={{0,4},{8,12},{16,20},{24,28},{32,36},{40,44},{48,52},{56,60},{64,6... | collective-permute-start | bytes 700424 | tf_op jit(solution)/shard_map/ppermute | solution.py:352
  29.5 16.1 %collective-permute-start.6 = (f32[256,384]{1,0:T(8,128)S(1)}, f32[256,384]{1,0:T(8,128)S(1)}, u32[]{:S(2)}, u32[]{:S(2)}) collective-permute-start(f32[256,384]{1,0:T(8,128)S(1)} %copy-done.5), channel_id=1, source_target_pairs={{0,2},{4,6},{8,10},{12,14},{16,18},{20,22},{24,26},{28,30},{32,34}... | collective-permute-start | bytes 1179656 | tf_op jit(solution)/shard_map/ppermute | solution.py:358
  30.9 37.2 %collective-permute-start.4 = (f32[456,128]{1,0:T(8,128)S(1)}, f32[456,128]{1,0:T(8,128)S(1)}, u32[]{:S(2)}, u32[]{:S(2)}) collective-permute-start(f32[456,128]{1,0:T(8,128)S(1)} %broadcast_select_fusion.5), channel_id=1, source_target_pairs={{0,2},{4,6},{8,10},{12,14},{16,18},{20,22},{24,26},{28,30},{32,34}... | collective-permute-start | bytes 700424 | tf_op jit(solution)/shard_map/ppermute | solution.py:358
  45.7 23.9 %collective-permute-start.7 = (f32[256,384]{1,0:T(8,128)S(1)}, f32[256,384]{1,0:T(8,128)S(1)}, u32[]{:S(2)}, u32[]{:S(2)}) collective-permute-start(f32[256,384]{1,0:T(8,128)S(1)} %broadcast_select_fusion), channel_id=1, source_target_pairs={{0,1},{2,3},{4,5},{6,7},{8,9},{10,11},{12,13},{14,15},{16,17},{18,... | collective-permute-start | bytes 1179656 | tf_op jit(solution)/shard_map/ppermute | solution.py:363
  68.2 2.4 %collective-permute-start.5 = (f32[456,128]{1,0:T(8,128)S(1)}, f32[456,128]{1,0:T(8,128)S(1)}, u32[]{:S(2)}, u32[]{:S(2)}) collective-permute-start(f32[456,128]{1,0:T(8,128)S(1)} %broadcast_select_fusion.6), channel_id=1, source_target_pairs={{0,1},{2,3},{4,5},{6,7},{8,9},{10,11},{12,13},{14,15},{16,17},{18,... | collective-permute-start | bytes 700424 | tf_op jit(solution)/shard_map/ppermute | solution.py:363
  71.3 4.8 %copy-start.2 = (s32[1,32]{1,0:T(1,128)S(1)}, s32[1,32]{1,0:T(1,128)}, u32[]{:S(2)}) copy-start(s32[1,32]{1,0:T(1,128)} %maps.3) | copy-start | bytes 388
  82.1 8.7 %collective-permute-start.12 = (f32[64,1024]{1,0:T(8,128)S(1)}, f32[64,1024]{1,0:T(8,128)S(1)}, u32[]{:S(2)}, u32[]{:S(2)}) collective-permute-start(f32[64,1024]{1,0:T(8,128)S(1)} %get-tuple-element.35), channel_id=1, source_target_pairs={{0,64},{64,0},{128,192},{192,128},{1,65},{65,1},{129,193},{193,129... | collective-permute-start | bytes 786440 | tf_op jit(solution)/shard_map/ppermute | solution.py:390
  83.7 10.2 %collective-permute-start.15 = (f32[64,1024]{1,0:T(8,128)S(1)}, f32[64,1024]{1,0:T(8,128)S(1)}, u32[]{:S(2)}, u32[]{:S(2)}) collective-permute-start(f32[64,1024]{1,0:T(8,128)S(1)} %get-tuple-element.37), channel_id=1, source_target_pairs={{0,192},{192,0},{64,128},{128,64},{1,193},{193,1},{65,129},{129,65... | collective-permute-start | bytes 786440 | tf_op jit(solution)/shard_map/ppermute | solution.py:390
  90.8 9.1 %collective-permute-start.13 = (f32[64,1024]{1,0:T(8,128)S(1)}, f32[64,1024]{1,0:T(8,128)S(1)}, u32[]{:S(2)}, u32[]{:S(2)}) collective-permute-start(f32[64,1024]{1,0:T(8,128)S(1)} %add.47), channel_id=1, source_target_pairs={{0,192},{192,0},{64,128},{128,64},{1,193},{193,1},{65,129},{129,65... | collective-permute-start | bytes 786440 | tf_op jit(solution)/shard_map/ppermute | solution.py:390
  93.8 10.7 %copy-start = (f32[1,256,1024]{2,1,0:T(8,128)S(1)}, f32[1,256,1024]{2,1,0:T(8,128)}, u32[]{:S(2)}) copy-start(f32[1,256,1024]{2,1,0:T(8,128)} %front.5) | copy-start | bytes 3145732
  93.8 10.7 %copy-start.1 = (f32[256,256]{1,0:T(8,128)S(1)}, f32[256,256]{1,0:T(8,128)}, u32[]{:S(2)}) copy-start(f32[256,256]{1,0:T(8,128)} %get-tuple-element.29.k_inv) | copy-start | bytes 786436
  93.8 10.7 %copy-start.3 = (f32[256,384]{1,0:T(8,128)S(1)}, f32[256,384]{1,0:T(8,128)}, u32[]{:S(2)}) copy-start(f32[256,384]{1,0:T(8,128)} %get-tuple-element.23.b_rows) | copy-start | bytes 1179652
  93.8 10.7 %copy-start.4 = (f32[256,256]{1,0:T(8,128)S(1)}, f32[256,256]{1,0:T(8,128)}, u32[]{:S(2)}) copy-start(f32[256,256]{1,0:T(8,128)} %get-tuple-element.28.k) | copy-start | bytes 786436
  93.9 7.6 %collective-permute-start.16 = (f32[64,1024]{1,0:T(8,128)S(1)}, f32[64,1024]{1,0:T(8,128)}, u32[]{:S(2)}, u32[]{:S(2)}) collective-permute-start(f32[64,1024]{1,0:T(8,128)S(1)} %add.49), channel_id=1, source_target_pairs={{0,64},{64,0},{128,192},{192,128},{1,65},{65,1},{129,193},{193,129... | collective-permute-start | bytes 786440 | tf_op jit(solution)/shard_map/ppermute | solution.py:390
  100.5 8.4 %collective-permute-start.14 = (f32[64,1024]{1,0:T(8,128)}, f32[64,1024]{1,0:T(8,128)}, u32[]{:S(2)}, u32[]{:S(2)}) collective-permute-start(f32[64,1024]{1,0:T(8,128)} %add.48), channel_id=1, source_target_pairs={{0,64},{64,0},{128,192},{192,128},{1,65},{65,1},{129,193},{193,129... | collective-permute-start | bytes 786440 | tf_op jit(solution)/shard_map/ppermute | solution.py:390
  102.5 7.9 %collective-permute-start.17 = (f32[64,1024]{1,0:T(8,128)S(1)}, f32[64,1024]{1,0:T(8,128)S(1)}, u32[]{:S(2)}, u32[]{:S(2)}) collective-permute-start(f32[64,1024]{1,0:T(8,128)S(1)} %add.50), channel_id=1, source_target_pairs={{0,192},{192,0},{64,128},{128,64},{1,193},{193,1},{65,129},{129,65... | collective-permute-start | bytes 786440 | tf_op jit(solution)/shard_map/ppermute | solution.py:390
  (1 other events, 1.6 us)
